TPU v7x, 256 devices: a whole 4x4x8 slice. The times are simulated.
256 devices in a mesh: src: 64 (over y, z, core), tgt: 4 (over x).
Axes of the slice: x: 4, y: 4, z: 8, core: 2. Of those that a mesh axis runs over, the one named last changes fastest.
Arguments:
- text_emb: bfloat16 [131072, 512], P('src'), may hold values from -32 to 32
- image_emb: bfloat16 [8192, 512], P('tgt'), may hold values from -12 to 12
- log_mass_src: float32 [131072], P('src'), may hold values from -1 to 1
- log_mass_tgt: float32 [8192], P('tgt'), may hold values from -1 to 1
- pair_blocks: int32 [4096, 2], P(('src', 'tgt')), may hold values from 0 to 7, as said below
- pair_counts: int32 [256], P(('src', 'tgt')), may hold values from 2 to 16, as said below
Outputs:
- src_map: float32 [131072, 512], P(('src', 'tgt'))
- tgt_map: float32 [8192, 512], P(('tgt', 'src'))
Inputs may be any that keep to these rules, and one draw needn't show every extreme that they name: `pair_blocks`: column 0 is a local text cluster below 8, column 1 a local image cluster below 8. The first pair_counts slots of a device hold distinct pairs; every text cluster and every image cluster lies in some used slot. Unused slots hold valid indices that are ignored. `pair_counts`: at least 8 // 4 used slots on every device; some device uses all 16 in every draw.
All inputs are finite; a program needn't handle non-finite values.
Results may differ from a plain program's by a relative error of at most 0.0028.
Values sent between devices are 32-bit elements; how exact they have to be, the bound alone decides.
No kernel may reach another device: no remote copies, remote signals or barrier semaphores. Data moves between devices by JAX's collectives and lax.ppermute only.
A program may use at most 64 MiB of HBM per device.

v0:
```python
import functools

import jax
import jax.numpy as jnp
from jax import lax
from jax.experimental import pallas as pl
from jax.experimental.pallas import tpu as pltpu
from jax.sharding import Mesh, PartitionSpec as P


BLK = 256
ITERS = 3
NB = 8
CAP = 16
D = 512
NX, NY, NZ, NC = 4, 4, 8, 2
FLOOR = -1e30
INV_TEMP = 0.15
STEP = 64


VMEM = pl.BlockSpec(memory_space=pltpu.VMEM)
SMEM = pl.BlockSpec(memory_space=pltpu.SMEM)
HBM = pl.BlockSpec(memory_space=pltpu.HBM)
f32 = jnp.float32


def lse_of(parts):
    peak = functools.reduce(jnp.maximum, parts)
    total = sum(jnp.exp(p - peak) for p in parts)
    return peak + jnp.log(total)


def lse_stack(ref):
    peak = jnp.max(ref[...], axis=0)
    total = jnp.sum(jnp.exp(ref[...] - peak[None]), axis=0)
    return peak + jnp.log(total)


def slots(cnt, pairs, body):
    def step(k, _):
        pair = pairs[k]
        body(k, pair // NB, pair % NB)
        return 0

    lax.fori_loop(0, cnt[0], step, 0)


def every_slot(cnt, act):
    def step(k, _):
        act(k)
        return 0

    lax.fori_loop(0, cnt[0], step, 0)


def fetch_scores(cnt, held, scores, sem):
    every_slot(cnt, lambda k: pltpu.make_async_copy(held.at[k], scores.at[k], sem.at[k]).start())
    return lambda k: pltpu.make_async_copy(held.at[k], scores.at[k], sem.at[k]).wait()


def fetch_blocks(held, out, sem):
    copies = [
        pltpu.make_async_copy(held.at[pl.ds(i * BLK, BLK), :], out.at[i], sem.at[i])
        for i in range(NB)
    ]
    for copy in copies:
        copy.start()
    return copies


def to_columns(rows):
    padded = jnp.concatenate([rows, jnp.zeros((120, BLK), f32)], axis=0)
    return jnp.transpose(padded)


def spread_columns(rows, out):
    cols = to_columns(rows)
    for a in range(NB):
        out[a] = jnp.broadcast_to(cols[:, a : a + 1], (BLK, 128))


def columns_to_rows(columns):
    lane = lax.broadcasted_iota(jnp.int32, (BLK, 128), 1)
    table = jnp.zeros((BLK, 128), f32)
    for a in range(NB):
        table = jnp.where(lane == a, columns[a], table)
    return jnp.transpose(table)[:NB]


def row_totals(cnt, pairs, scores, v, m_ref, s_ref, lse_out):
    for a in range(NB):
        m_ref[a] = jnp.broadcast_to(jnp.max(m_ref[a], axis=1, keepdims=True), (BLK, 128))
        s_ref[a] = jnp.zeros((BLK, 128), f32)

    def body(k, a, b):
        shift = v[pl.ds(b, 1), :] if v is not None else None
        for r in range(0, BLK, STEP):
            rows = slice(r, r + STEP)
            tile = scores[k, rows, :]
            if shift is not None:
                tile = tile + shift
            peak = m_ref[a, rows, :]
            s_ref[a, rows, :] += jnp.exp(tile[:, :128] - peak) + jnp.exp(tile[:, 128:] - peak)

    slots(cnt, pairs, body)
    columns = []
    for a in range(NB):
        total = jnp.sum(s_ref[a], axis=1, keepdims=True)
        value = jnp.where(total > 0, m_ref[a, :, :1] + jnp.log(total), FLOOR)
        columns.append(jnp.broadcast_to(value, (BLK, 128)))
    lse_out[...] = columns_to_rows(columns)


def first_kernel(
    cnt, pairs, text, image, held, lse_out, m_ref, s_ref, scores, texts, images, sem, tsem, isem
):
    copies = fetch_blocks(text, texts, tsem) + fetch_blocks(image, images, isem)
    m_ref[...] = jnp.full(m_ref.shape, FLOOR, f32)
    for copy in copies:
        copy.wait()

    def body(k, a, b):
        tile = (
            lax.dot_general(
                texts[a], images[b], (((1,), (1,)), ((), ())), preferred_element_type=f32
            )
            * INV_TEMP
        )
        scores[k] = tile
        m_ref[a] = jnp.maximum(m_ref[a], jnp.maximum(tile[:, :128], tile[:, 128:]))

    slots(cnt, pairs, body)
    every_slot(cnt, lambda k: pltpu.make_async_copy(scores.at[k], held.at[k], sem.at[k]).start())
    row_totals(cnt, pairs, scores, None, m_ref, s_ref, lse_out)
    every_slot(cnt, lambda k: pltpu.make_async_copy(scores.at[k], held.at[k], sem.at[k]).wait())


def row_kernel(cnt, pairs, held, parts, mass, lse_out, v_ref, m_ref, s_ref, scores, sem):
    arrive = fetch_scores(cnt, held, scores, sem)
    v_ref[...] = mass[...] - lse_stack(parts)
    m_ref[...] = jnp.full(m_ref.shape, FLOOR, f32)

    def body(k, a, b):
        arrive(k)
        shift = v_ref[pl.ds(b, 1), :]
        for r in range(0, BLK, STEP):
            rows = slice(r, r + STEP)
            tile = scores[k, rows, :] + shift
            m_ref[a, rows, :] = jnp.maximum(
                m_ref[a, rows, :], jnp.maximum(tile[:, :128], tile[:, 128:])
            )

    slots(cnt, pairs, body)
    row_totals(cnt, pairs, scores, v_ref, m_ref, s_ref, lse_out)


def col_peaks(cnt, pairs, scores, arrive, u, u_ref, m_ref, s_ref):
    spread_columns(u, u_ref)
    m_ref[...] = jnp.full(m_ref.shape, FLOOR, f32)
    s_ref[...] = jnp.zeros(s_ref.shape, f32)

    def peaks(k, a, b):
        arrive(k)
        for half in range(2):
            lanes = slice(half * 128, half * 128 + 128)
            best = m_ref[b, :, lanes]
            for r in range(0, BLK, STEP):
                tile = scores[k, r : r + STEP, lanes] + u_ref[a, r : r + STEP, :]
                best = jnp.maximum(best, jnp.max(tile.reshape(STEP // 8, 8, 128), axis=0))
            m_ref[b, :, lanes] = best

    slots(cnt, pairs, peaks)
    for b in range(NB):
        m_ref[b] = jnp.broadcast_to(jnp.max(m_ref[b], axis=0, keepdims=True), (8, BLK))


def col_lse(m_ref, s_ref, lse_out):
    totals = []
    for b in range(NB):
        total = jnp.sum(s_ref[b], axis=0, keepdims=True)
        lse_out[b : b + 1, :] = jnp.where(total > 0, m_ref[b, :1, :] + jnp.log(total), FLOOR)
        totals.append(total)
    return totals


def col_kernel(
    cnt, pairs, held, p0, p1, p2, p3, mass, lse_out, u_ref, m_ref, s_ref, scores, sem
):
    arrive = fetch_scores(cnt, held, scores, sem)
    u = mass[...] - lse_of([p0[...], p1[...], p2[...], p3[...]])
    col_peaks(cnt, pairs, scores, arrive, u, u_ref, m_ref, s_ref)

    def totals(k, a, b):
        for half in range(2):
            lanes = slice(half * 128, half * 128 + 128)
            peak = m_ref[b, :, lanes]
            total = s_ref[b, :, lanes]
            for r in range(0, BLK, STEP):
                tile = scores[k, r : r + STEP, lanes] + u_ref[a, r : r + STEP, :]
                tile = jnp.exp(tile.reshape(STEP // 8, 8, 128) - peak[None])
                total = total + jnp.sum(tile, axis=0)
            s_ref[b, :, lanes] = total

    slots(cnt, pairs, totals)
    col_lse(m_ref, s_ref, lse_out)


def last_col_kernel(
    cnt, pairs, place, held, p0, p1, p2, p3, mass, text, lse_out, u_out, keep, send,
    u_ref, m_ref, s_ref, scores, sem, texts, tsem, hi_ref, lo_ref, acc,
):
    arrive = fetch_scores(cnt, held, scores, sem)
    copies = fetch_blocks(text, texts, tsem)
    u = mass[...] - lse_of([p0[...], p1[...], p2[...], p3[...]])
    u_out[...] = u
    col_peaks(cnt, pairs, scores, arrive, u, u_ref, m_ref, s_ref)
    acc[...] = jnp.zeros(acc.shape, f32)
    for copy in copies:
        copy.wait()

    def totals(k, a, b):
        for half in range(2):
            lanes = slice(half * 128, half * 128 + 128)
            peak = m_ref[b, :, lanes]
            total = s_ref[b, :, lanes]
            for r in range(0, BLK, STEP):
                tile = scores[k, r : r + STEP, lanes] + u_ref[a, r : r + STEP, :]
                tile = jnp.exp(tile.reshape(STEP // 8, 8, 128) - peak[None])
                total = total + jnp.sum(tile, axis=0)
                tile = tile.reshape(STEP, 128)
                high = tile.astype(jnp.bfloat16)
                hi_ref[r : r + STEP, lanes] = high
                lo_ref[r : r + STEP, lanes] = (tile - high.astype(f32)).astype(jnp.bfloat16)
            s_ref[b, :, lanes] = total
        rows = texts[a]
        dims = (((0,), (0,)), ((), ()))
        acc[b] += lax.dot_general(
            hi_ref[...], rows, dims, preferred_element_type=f32
        ) + lax.dot_general(lo_ref[...], rows, dims, preferred_element_type=f32)

    slots(cnt, pairs, totals)
    sums = jnp.concatenate(col_lse(m_ref, s_ref, lse_out), axis=0)
    spread_columns(jnp.where(sums > 0, 1.0 / sums, 0.0), u_ref)
    y, c = place[1], place[2]
    for r in range(NY):
        b0 = 2 * lax.rem(y + r, NY)
        for z in range(NZ):
            b = b0 + z // 4
            for out, core in ((keep, c), (send, 1 - c)):
                rows = pl.ds(pl.multiple_of((z % 4) * 64 + core * 32, 32), 32)
                scale = u_ref[b, rows, :]
                for q in range(0, D, 128):
                    out[r, z, :, q : q + 128] = acc[b, rows, q : q + 128] * scale


def scale_kernel(place, parts, mass, mine, other, keep, got, after, *refs):
    outs = refs[:8]
    f0_ref, f1_ref = refs[8:]
    v = mass[...] - lse_stack(parts)
    total = jnp.sum(jnp.exp(parts[...] + v[None]), axis=0)
    spread_columns(jnp.exp(mine[...] + v) / total, f0_ref)
    spread_columns(jnp.exp(other[...] + v) / total, f1_ref)
    y, c = place[1], place[2]
    for r in range(NY):
        b0 = 2 * lax.rem(y + r, NY)
        for z in range(NZ):
            b = b0 + z // 4
            rows = pl.ds(pl.multiple_of((z % 4) * 64 + c * 32, 32), 32)
            f0, f1 = f0_ref[b, rows, :], f1_ref[b, rows, :]
            for q in range(0, D, 128):
                lanes = slice(q, q + 128)
                outs[2 * r + z // 4][z % 4, :, lanes] = (
                    keep[r, z, :, lanes] * f0 + got[r, z, :, lanes] * f1
                )


def final_kernel(cnt, pairs, place, held, parts, mass, u, image, *refs):
    src_out = refs[:8]
    scores, sem, images, isem, v_ref, u_ref, w_ref, src_acc, rsum, rmass = refs[8:]
    arrive = fetch_scores(cnt, held, scores, sem)
    copies = fetch_blocks(image, images, isem)
    v_ref[...] = mass[...] - lse_stack(parts)
    spread_columns(u[...], u_ref)
    src_acc[...] = jnp.zeros(src_acc.shape, f32)
    rsum[...] = jnp.zeros(rsum.shape, f32)
    for copy in copies:
        copy.wait()

    def body(k, a, b):
        arrive(k)
        v = v_ref[pl.ds(b, 1), :]
        for r in range(0, BLK, STEP):
            rows = slice(r, r + STEP)
            for half in range(2):
                lanes = slice(half * 128, half * 128 + 128)
                plan = jnp.exp(scores[k, rows, lanes] + u_ref[a, rows, :] + v[:, lanes])
                rsum[a, rows, :] += plan
                w_ref[rows, lanes] = plan.astype(jnp.bfloat16)
        src_acc[a] += jnp.dot(
            w_ref[...], images[b], preferred_element_type=f32
        )

    slots(cnt, pairs, body)
    rmass[...] = columns_to_rows(
        [
            jnp.broadcast_to(jnp.sum(rsum[a], axis=1, keepdims=True), (BLK, 128))
            for a in range(NB)
        ]
    )
    x = place[0]
    for r in range(NB):
        a = lax.rem(2 * x + r, NB)
        src_out[r][:BLK, :] = src_acc[a]
        src_out[r][BLK:, :BLK] = jnp.broadcast_to(rmass[pl.ds(a, 1), :], (8, BLK))
        src_out[r][BLK:, BLK:] = jnp.zeros((8, D - BLK), f32)


def src_norm_kernel(own, plus, minus, out):
    total = own[...] + plus[...] + minus[...]
    cols = to_columns(total[BLK:, :BLK])
    out[...] = total[:BLK, :] / cols[:, :1]


def call(kernel, outs, args, smem, scratch=(), mib=50, hbm=(), flops=1 << 24):
    n = len(args)
    specs = [SMEM if i < smem else HBM if i in hbm else VMEM for i in range(n)]
    flat, tree = jax.tree.flatten(outs)
    out_specs = tree.unflatten([HBM if n + i in hbm else VMEM for i in range(len(flat))])
    return pl.pallas_call(
        kernel,
        out_shape=outs,
        in_specs=specs,
        out_specs=out_specs,
        scratch_shapes=list(scratch),
        compiler_params=pltpu.CompilerParams(vmem_limit_bytes=mib << 20),
        cost_estimate=pl.CostEstimate(
            flops=flops, bytes_accessed=8 << 20, transcendentals=CAP * BLK * BLK
        ),
    )(*args)


def sds(*shape):
    return jax.ShapeDtypeStruct(shape, f32)


def shift(a, axis, size, by):
    return lax.ppermute(a, axis, [(i, (i + by) % size) for i in range(size)])


def over_x(part):
    return [part] + [shift(part, "x", NX, k) for k in (1, 3, 2)]


def over_src(part):
    other = shift(part, "c", NC, 1)
    both = lse_of([part, other])
    copies = jnp.broadcast_to(both[None], (NY * NZ, NB, BLK))
    return lax.all_to_all(copies, ("y", "z"), 0, 0, tiled=True), other


def ring_scatter(own_a, own_b, plus_a, plus_b, far_a, far_b, minus_a, minus_b, axis, size):
    def move(value, by):
        return shift(value, axis, size, by)

    relay_up = move(far_a, 1)
    relay_down = move(far_b, -1)
    from_below_b = move(plus_b, 1)
    from_above_a = move(minus_a, -1)
    from_below_a = move(plus_a + relay_up, 1)
    from_above_b = move(minus_b + relay_down, -1)
    return (own_a, from_below_a, from_above_a), (own_b, from_below_b, from_above_b)


def program(text, image, log_mass_src, log_mass_tgt, pairs, count):
    mass_src = log_mass_src.reshape(NB, BLK)
    mass_tgt = log_mass_tgt.reshape(NB, BLK)
    pairs = pairs[:, 0] * NB + pairs[:, 1]
    place = jnp.stack([lax.axis_index("x"), lax.axis_index("y"), lax.axis_index("c")])
    row_scratch = [pltpu.VMEM((NB, BLK, 128), f32)] * 2
    col_scratch = [pltpu.VMEM((NB, BLK, 128), f32)] + [pltpu.VMEM((NB, 8, BLK), f32)] * 2
    tiles = [pltpu.VMEM((CAP, BLK, BLK), f32), pltpu.SemaphoreType.DMA((CAP,))]
    blocks = [pltpu.VMEM((NB, BLK, D), jnp.bfloat16)]
    block_sem = [pltpu.SemaphoreType.DMA((NB,))]
    stats = sds(NB, BLK)
    scores, part = call(
        first_kernel,
        (sds(CAP, BLK, BLK), stats),
        (count, pairs, text, image),
        2,
        row_scratch + tiles[:1] + blocks * 2 + tiles[1:] + block_sem * 2,
        52,
        (2, 3, 4),
        1 << 30,
    )
    for _ in range(ITERS - 1):
        part = call(
            col_kernel,
            stats,
            (count, pairs, scores, *over_x(part), mass_src),
            2,
            col_scratch + tiles,
            hbm=(2,),
        )
        stack, _ = over_src(part)
        part = call(
            row_kernel,
            stats,
            (count, pairs, scores, stack, mass_tgt),
            2,
            [pltpu.VMEM((NB, BLK), f32)] + row_scratch + tiles,
            hbm=(2,),
        )
    half = sds(NY, NZ, 32, D)
    mine, u, keep, send = call(
        last_col_kernel,
        (stats, stats, half, half),
        (count, pairs, place, scores, *over_x(part), mass_src, text),
        3,
        col_scratch
        + tiles
        + blocks
        + block_sem
        + [pltpu.VMEM((BLK, BLK), jnp.bfloat16)] * 2
        + [pltpu.VMEM((NB, BLK, D), f32)],
        50,
        (3, 9),
        1 << 31,
    )
    stack, other = over_src(mine)
    got = shift(send, "c", NC, 1)
    outs = call(
        final_kernel,
        tuple([sds(BLK + 8, D)] * 8),
        (count, pairs, place, scores, stack, mass_tgt, u, image),
        3,
        tiles
        + blocks
        + block_sem
        + [
            pltpu.VMEM((NB, BLK), f32),
            pltpu.VMEM((NB, BLK, 128), f32),
            pltpu.VMEM((BLK, BLK), jnp.bfloat16),
            pltpu.VMEM((NB, BLK, D), f32),
            pltpu.VMEM((NB, BLK, 128), f32),
            pltpu.VMEM((NB, BLK), f32),
        ],
        50,
        (3, 7),
        1 << 30,
    )
    halves = call(
        scale_kernel,
        tuple([sds(4, 32, D)] * 8),
        (place, stack, mass_tgt, mine, other, keep, got, outs[4]),
        1,
        [pltpu.VMEM((NB, BLK, 128), f32)] * 2,
        16,
        (7,),
    )
    part_a, part_b = ring_scatter(*outs, "x", NX)
    tgt_a, tgt_b = ring_scatter(*halves, "y", NY)
    summed = jnp.concatenate([sum(tgt_a), sum(tgt_b)], axis=0)
    got = lax.all_to_all(summed, "z", 0, 0, tiled=True)
    tgt_map = jnp.sum(got, axis=0)
    src_map = jnp.concatenate(
        [call(src_norm_kernel, sds(BLK, D), p, 0, (), 16) for p in (part_a, part_b)],
        axis=0,
    )
    return (src_map, tgt_map.reshape(32, D))


def solution(mesh):
    grid = Mesh(mesh.devices.reshape(NY, NZ, NC, NX), ("y", "z", "c", "x"))
    src = ("y", "z", "c")
    return jax.shard_map(
        program,
        mesh=grid,
        in_specs=(P(src, None), P("x", None), P(src), P("x"), P((*src, "x"), None), P((*src, "x"))),
        out_specs=(P((*src, "x"), None), P(("x", *src), None)),
        check_vma=False,
    )
```

profile of v0, /device:TPU:1, one launch (start us, length us, event | category | flops | bytes accessed | tf_op | source)
XLA Modules:
  0.0 195.3 jit_solution(17341973451536469273)
XLA Ops:
  1.3 0.8 add_bitcast_fusion.pairs
  2.0 4.7 %shard_map.77 = (f32[16,256,256]{2,1,0:T(8,128)}, f32[8,256]{1,0:T(8,128)S(1)}) custom-call(s32[1]{0:T(128)S(6)} %copy.8.cnt, s32[16]{0:T(128)S(1)} %add_bitcast_fusion.pairs, bf16[2048,512]{1,0:T(8,128)(2,1)} %text.3, bf16[2048,512]{1,0:T(8,128)(2,1)} %image.3), custom_call_target="tpu_custom_call" | custom-call | flops 1073741824 | bytes 8388608 | tf_op jit(solution)/shard_map/pallas_call | solution.py:330
  6.7 6.0 %collective-permute-start.2 = (f32[8,256]{1,0:T(8,128)S(1)}, f32[8,256]{1,0:T(8,128)S(1)}, u32[]{:S(2)}, u32[]{:S(2)}) collective-permute-start(f32[8,256]{1,0:T(8,128)S(1)} %get-tuple-element.25.p0), channel_id=1, source_target_pairs={{0,2},{1,3},{2,0},{3,1},{4,6},{5,7},{6,4},{7,5},{8,10},{9,11},{10,... | collective-permute-start | bytes 24584 | tf_op jit(solution)/shard_map/ppermute | solution.py:348
  12.7 1.5 collective-permute-start
  14.2 1.0 collective-permute-done.1.p2
  15.2 1.2 collective-permute-done.p1
  16.4 1.9 shard_map.78
  18.3 7.7 %collective-permute-start.3 = (f32[8,256]{1,0:T(8,128)S(1)}, f32[8,256]{1,0:T(8,128)S(1)}, u32[]{:S(2)}, u32[]{:S(2)}) collective-permute-start(f32[8,256]{1,0:T(8,128)S(1)} %shard_map.78), channel_id=1, source_target_pairs={{0,4},{4,0},{1,5},{5,1},{2,6},{6,2},{3,7},{7,3},{8,12},{12,8},{9,1... | collective-permute-start | bytes 24584 | tf_op jit(solution)/shard_map/ppermute | solution.py:348
  26.0 0.8 collective-permute-done.3
  26.9 0.7 broadcast_in_dim.6
  27.6 9.1 %all-to-all-start = ((f32[32,8,256]{2,1,0:T(8,128)}), f32[32,8,256]{2,1,0:T(8,128)S(1)}, u32[]{:S(2)}, u32[]{:S(2)}) async-start(f32[32,8,256]{2,1,0:T(8,128)} %broadcast_in_dim.6), calls=%async_computation | async-start | bytes 524288 | tf_op jit(solution)/shard_map/all_to_all | solution.py:359
  36.8 10.1 %all-to-all-done.parts = f32[32,8,256]{2,1,0:T(8,128)S(1)} async-done(((f32[32,8,256]{2,1,0:T(8,128)}), f32[32,8,256]{2,1,0:T(8,128)S(1)}, u32[]{:S(2)}, u32[]{:S(2)}) %all-to-all-start) | async-done | bytes 262176 | tf_op jit(solution)/shard_map/all_to_all | solution.py:359
  46.8 2.9 %shard_map.79.p0 = f32[8,256]{1,0:T(8,128)S(1)} custom-call(s32[1]{0:T(128)S(6)} %copy.8.cnt, s32[16]{0:T(128)S(1)} %add_bitcast_fusion.pairs, f32[16,256,256]{2,1,0:T(8,128)} %get-tuple-element.24.held, f32[32,8,256]{2,1,0:T(8,128)S(1)} %all-to-all-done.parts, f32[8,256]{1,0:T(8,128)S(1)} %reshape.17.mass), custom_call_target="tpu_custom_call" | custom-call | flops 16777216 | bytes 8388608 | tf_op jit(solution)/shard_map/pallas_call | solution.py:330
  49.7 2.1 %collective-permute-start.6 = (f32[8,256]{1,0:T(8,128)S(1)}, f32[8,256]{1,0:T(8,128)S(1)}, u32[]{:S(2)}, u32[]{:S(2)}) collective-permute-start(f32[8,256]{1,0:T(8,128)S(1)} %shard_map.79.p0), channel_id=1, source_target_pairs={{0,2},{1,3},{2,0},{3,1},{4,6},{5,7},{6,4},{7,5},{8,10},{9,11},{10,... | collective-permute-start | bytes 24584 | tf_op jit(solution)/shard_map/ppermute | solution.py:348
  51.9 1.5 collective-permute-start.4
  54.4 1.2 collective-permute-done.4.p1
  55.6 1.9 shard_map.80
  57.5 9.0 %collective-permute-start.7 = (f32[8,256]{1,0:T(8,128)S(1)}, f32[8,256]{1,0:T(8,128)S(1)}, u32[]{:S(2)}, u32[]{:S(2)}) collective-permute-start(f32[8,256]{1,0:T(8,128)S(1)} %shard_map.80), channel_id=1, source_target_pairs={{0,4},{4,0},{1,5},{5,1},{2,6},{6,2},{3,7},{7,3},{8,12},{12,8},{9,1... | collective-permute-start | bytes 24584 | tf_op jit(solution)/shard_map/ppermute | solution.py:348
  66.5 0.8 collective-permute-done.7
  68.1 3.9 %all-to-all-start.1 = ((f32[32,8,256]{2,1,0:T(8,128)}), f32[32,8,256]{2,1,0:T(8,128)S(1)}, u32[]{:S(2)}, u32[]{:S(2)}) async-start(f32[32,8,256]{2,1,0:T(8,128)} %broadcast_in_dim.7), calls=%async_computation.1 | async-start | bytes 524288 | tf_op jit(solution)/shard_map/all_to_all | solution.py:359
  72.0 10.3 %all-to-all-done.1.parts = f32[32,8,256]{2,1,0:T(8,128)S(1)} async-done(((f32[32,8,256]{2,1,0:T(8,128)}), f32[32,8,256]{2,1,0:T(8,128)S(1)}, u32[]{:S(2)}, u32[]{:S(2)}) %all-to-all-start.1) | async-done | bytes 262176 | tf_op jit(solution)/shard_map/all_to_all | solution.py:359
  82.2 2.9 %shard_map.81.p0 = f32[8,256]{1,0:T(8,128)S(1)} custom-call(s32[1]{0:T(128)S(6)} %copy.8.cnt, s32[16]{0:T(128)S(1)} %add_bitcast_fusion.pairs, f32[16,256,256]{2,1,0:T(8,128)} %get-tuple-element.24.held, f32[32,8,256]{2,1,0:T(8,128)S(1)} %all-to-all-done.1.parts, f32[8,256]{1,0:T(8,128)S(1)} %reshape.17.mass), custom_call_target="tpu_custom_call" | custom-call | flops 16777216 | bytes 8388608 | tf_op jit(solution)/shard_map/pallas_call | solution.py:330
  86.0 1.1 collective-permute-start.8
  87.1 2.1 %collective-permute-done.10.p3 = f32[8,256]{1,0:T(8,128)S(1)} collective-permute-done((f32[8,256]{1,0:T(8,128)S(1)}, f32[8,256]{1,0:T(8,128)S(1)}, u32[]{:S(2)}, u32[]{:S(2)}) %collective-permute-start.10) | collective-permute-done | bytes 8224 | tf_op jit(solution)/shard_map/ppermute | solution.py:348
  89.7 5.5 %shard_map.82 = (f32[8,256]{1,0:T(8,128)S(1)}, f32[8,256]{1,0:T(8,128)S(1)}, f32[4,8,32,512]{3,2,1,0:T(8,128)S(1)}, f32[4,8,32,512]{3,2,1,0:T(8,128)}) custom-call(s32[1]{0:T(128)S(6)} %copy.8.cnt, s32[16]{0:T(128)S(1)} %add_bitcast_fusion.pairs, s32[3]{0:T(128)S(1)} %pad_add_fusion.place, f32[16,256,256]{2,1,0:T(8,128)} %get-tuple-element.24.held, ...), custom_call_target="tpu_custom_call" | custom-call | flops 2147483648 | bytes 8388608 | tf_op jit(solution)/shard_map/pallas_call | solution.py:330
  95.2 14.3 %collective-permute-start.18 = (f32[4,8,32,512]{3,2,1,0:T(8,128)}, f32[4,8,32,512]{3,2,1,0:T(8,128)S(1)}, u32[]{:S(2)}, u32[]{:S(2)}) collective-permute-start(f32[4,8,32,512]{3,2,1,0:T(8,128)} %get-tuple-element.37), channel_id=1, source_target_pairs={{0,4},{4,0},{1,5},{5,1},{2,6},{6,2},{3,7},{7,3},{8,12},{12,8},{9,1... | collective-permute-start | bytes 6291464 | tf_op jit(solution)/shard_map/ppermute | solution.py:348
  109.6 3.9 %collective-permute-done.11.other = f32[8,256]{1,0:T(8,128)S(1)} collective-permute-done((f32[8,256]{1,0:T(8,128)S(1)}, f32[8,256]{1,0:T(8,128)S(1)}, u32[]{:S(2)}, u32[]{:S(2)}) %collective-permute-start.11) | collective-permute-done | bytes 8224 | tf_op jit(solution)/shard_map/ppermute | solution.py:348
  113.6 12.7 %all_to_all.20.parts = f32[32,8,256]{2,1,0:T(8,128)S(1)} all-to-all(f32[32,8,256]{2,1,0:T(8,128)S(1)} %broadcast_in_dim.8), channel_id=1, replica_groups=mesh['y'=4,'z'=8,'c'=2,'x'=4] {'y','z'}, dimensions={0} | all-to-all | bytes 524288 | tf_op jit(solution)/shard_map/all_to_all | solution.py:359
  126.3 4.8 %shard_map.83 = (f32[264,512]{1,0:T(8,128)S(1)}, f32[264,512]{1,0:T(8,128)S(1)}, f32[264,512]{1,0:T(8,128)S(1)}, f32[264,512]{1,0:T(8,128)S(1)}, f32[264,512]{1,...) custom-call(s32[1]{0:T(128)S(6)} %copy.8.cnt, s32[16]{0:T(128)S(1)} %add_bitcast_fusion.pairs, ...), custom_call_target="tpu_custom_call" | custom-call | flops 1073741824 | bytes 8388608 | tf_op jit(solution)/shard_map/pallas_call | solution.py:330
  131.1 1.9 shard_map.86
  133.0 5.1 %collective-permute-start.19 = (f32[4,32,512]{2,1,0:T(8,128)S(1)}, f32[4,32,512]{2,1,0:T(8,128)S(1)}, u32[]{:S(2)}, u32[]{:S(2)}) collective-permute-start(f32[4,32,512]{2,1,0:T(8,128)S(1)} %get-tuple-element.40), channel_id=1, source_target_pairs={{0,64},{64,128},{128,192},{192,0},{1,65},{65,129},{129,193},{193,1... | collective-permute-start | bytes 786440 | tf_op jit(solution)/shard_map/ppermute | solution.py:348
  138.2 3.3 %collective-permute-done.19 = f32[4,32,512]{2,1,0:T(8,128)S(1)} collective-permute-done((f32[4,32,512]{2,1,0:T(8,128)S(1)}, f32[4,32,512]{2,1,0:T(8,128)S(1)}, u32[]{:S(2)}, u32[]{:S(2)}) %collective-permute-start.19) | collective-permute-done | bytes 262176 | tf_op jit(solution)/shard_map/ppermute | solution.py:348
  141.5 2.0 %collective-permute-start.20 = (f32[4,32,512]{2,1,0:T(8,128)S(1)}, f32[4,32,512]{2,1,0:T(8,128)S(1)}, u32[]{:S(2)}, u32[]{:S(2)}) collective-permute-start(f32[4,32,512]{2,1,0:T(8,128)S(1)} %add.57), channel_id=1, source_target_pairs={{0,64},{64,128},{128,192},{192,0},{1,65},{65,129},{129,193},{193,1... | collective-permute-start | bytes 786440 | tf_op jit(solution)/shard_map/ppermute | solution.py:348
  143.7 2.7 %collective-permute-start.24 = (f32[4,32,512]{2,1,0:T(8,128)S(1)}, f32[4,32,512]{2,1,0:T(8,128)S(1)}, u32[]{:S(2)}, u32[]{:S(2)}) collective-permute-start(f32[4,32,512]{2,1,0:T(8,128)S(1)} %add.61), channel_id=1, source_target_pairs={{0,192},{64,0},{128,64},{192,128},{1,193},{65,1},{129,65},{193,129... | collective-permute-start | bytes 786440 | tf_op jit(solution)/shard_map/ppermute | solution.py:348
  146.3 1.5 collective-permute-done.21
  147.9 1.1 collective-permute-start.16
  149.0 1.9 collective-permute-done.20
  151.0 2.7 %collective-permute-done.22 = f32[4,32,512]{2,1,0:T(8,128)S(1)} collective-permute-done((f32[4,32,512]{2,1,0:T(8,128)S(1)}, f32[4,32,512]{2,1,0:T(8,128)S(1)}, u32[]{:S(2)}, u32[]{:S(2)}) %collective-permute-start.22) | collective-permute-done | bytes 262176 | tf_op jit(solution)/shard_map/ppermute | solution.py:348
  153.7 0.8 pad_maximum_fusion.1
  154.6 11.9 %all-to-all-start.3 = ((f32[8,32,512]{2,1,0:T(8,128)}), f32[8,32,512]{2,1,0:T(8,128)}, u32[]{:S(2)}, u32[]{:S(2)}) async-start(f32[8,32,512]{2,1,0:T(8,128)} %pad_maximum_fusion.1), calls=%async_computation.3 | async-start | bytes 1048576 | tf_op jit(solution)/shard_map/all_to_all | solution.py:464
  166.5 1.3 add.56
  167.8 2.7 %collective-permute-start.17 = (f32[264,512]{1,0:T(8,128)S(1)}, f32[264,512]{1,0:T(8,128)S(1)}, u32[]{:S(2)}, u32[]{:S(2)}) collective-permute-start(f32[264,512]{1,0:T(8,128)S(1)} %add.56), channel_id=1, source_target_pairs={{0,3},{1,0},{2,1},{3,2},{4,7},{5,4},{6,5},{7,6},{8,11},{9,8},{10,9... | collective-permute-start | bytes 1622024 | tf_op jit(solution)/shard_map/ppermute | solution.py:348
  170.6 1.1 add.55
  171.7 1.5 collective-permute-start.13
  173.2 7.2 %collective-permute-done.15.plus = f32[264,512]{1,0:T(8,128)S(1)} collective-permute-done((f32[264,512]{1,0:T(8,128)S(1)}, f32[264,512]{1,0:T(8,128)S(1)}, u32[]{:S(2)}, u32[]{:S(2)}) %collective-permute-start.15) | collective-permute-done | bytes 540704 | tf_op jit(solution)/shard_map/ppermute | solution.py:348
  181.0 11.3 %collective-permute-done.14.minus = f32[264,512]{1,0:T(8,128)S(1)} collective-permute-done((f32[264,512]{1,0:T(8,128)S(1)}, f32[264,512]{1,0:T(8,128)S(1)}, u32[]{:S(2)}, u32[]{:S(2)}) %collective-permute-start.14) | collective-permute-done | bytes 540704 | tf_op jit(solution)/shard_map/ppermute | solution.py:348
  192.6 1.0 pad_maximum_fusion
  193.6 1.7 reduce_sum.9
  (42 shorter events, 4.6 us)
Async XLA Ops:
  2.0 12.1 %copy-start = (f32[2048]{0:T(1024)S(1)}, f32[2048]{0:T(1024)}, u32[]{:S(2)}) copy-start(f32[2048]{0:T(1024)} %param.8) | copy-start | bytes 24580
  6.7 7.5 %collective-permute-start.2 = (f32[8,256]{1,0:T(8,128)S(1)}, f32[8,256]{1,0:T(8,128)S(1)}, u32[]{:S(2)}, u32[]{:S(2)}) collective-permute-start(f32[8,256]{1,0:T(8,128)S(1)} %get-tuple-element.25.p0), channel_id=1, source_target_pairs={{0,2},{1,3},{2,0},{3,1},{4,6},{5,7},{6,4},{7,5},{8,10},{9,11},{10,... | collective-permute-start | bytes 24584 | tf_op jit(solution)/shard_map/ppermute | solution.py:348
  12.7 2.5 %collective-permute-start.1 = (f32[8,256]{1,0:T(8,128)S(1)}, f32[8,256]{1,0:T(8,128)S(1)}, u32[]{:S(2)}, u32[]{:S(2)}) collective-permute-start(f32[8,256]{1,0:T(8,128)S(1)} %get-tuple-element.25.p0), channel_id=1, source_target_pairs={{0,3},{1,0},{2,1},{3,2},{4,7},{5,4},{6,5},{7,6},{8,11},{9,8},{10,9... | collective-permute-start | bytes 24584 | tf_op jit(solution)/shard_map/ppermute | solution.py:348
  12.7 3.7 %collective-permute-start = (f32[8,256]{1,0:T(8,128)S(1)}, f32[8,256]{1,0:T(8,128)S(1)}, u32[]{:S(2)}, u32[]{:S(2)}) collective-permute-start(f32[8,256]{1,0:T(8,128)S(1)} %get-tuple-element.25.p0), channel_id=1, source_target_pairs={{0,1},{1,2},{2,3},{3,0},{4,5},{5,6},{6,7},{7,4},{8,9},{9,10},{10,1... | collective-permute-start | bytes 24584 | tf_op jit(solution)/shard_map/ppermute | solution.py:348
  16.4 20.4 %copy-start.1 = (f32[2048]{0:T(1024)S(1)}, f32[2048]{0:T(1024)}, u32[]{:S(2)}) copy-start(f32[2048]{0:T(1024)} %param.9) | copy-start | bytes 24580
  18.3 8.5 %collective-permute-start.3 = (f32[8,256]{1,0:T(8,128)S(1)}, f32[8,256]{1,0:T(8,128)S(1)}, u32[]{:S(2)}, u32[]{:S(2)}) collective-permute-start(f32[8,256]{1,0:T(8,128)S(1)} %shard_map.78), channel_id=1, source_target_pairs={{0,4},{4,0},{1,5},{5,1},{2,6},{6,2},{3,7},{7,3},{8,12},{12,8},{9,1... | collective-permute-start | bytes 24584 | tf_op jit(solution)/shard_map/ppermute | solution.py:348
  27.6 19.2 %all-to-all-start = ((f32[32,8,256]{2,1,0:T(8,128)}), f32[32,8,256]{2,1,0:T(8,128)S(1)}, u32[]{:S(2)}, u32[]{:S(2)}) async-start(f32[32,8,256]{2,1,0:T(8,128)} %broadcast_in_dim.6), calls=%async_computation | async-start | bytes 524288 | tf_op jit(solution)/shard_map/all_to_all | solution.py:359
  49.7 4.1 %collective-permute-start.6 = (f32[8,256]{1,0:T(8,128)S(1)}, f32[8,256]{1,0:T(8,128)S(1)}, u32[]{:S(2)}, u32[]{:S(2)}) collective-permute-start(f32[8,256]{1,0:T(8,128)S(1)} %shard_map.79.p0), channel_id=1, source_target_pairs={{0,2},{1,3},{2,0},{3,1},{4,6},{5,7},{6,4},{7,5},{8,10},{9,11},{10,... | collective-permute-start | bytes 24584 | tf_op jit(solution)/shard_map/ppermute | solution.py:348
  51.9 2.5 %collective-permute-start.5 = (f32[8,256]{1,0:T(8,128)S(1)}, f32[8,256]{1,0:T(8,128)S(1)}, u32[]{:S(2)}, u32[]{:S(2)}) collective-permute-start(f32[8,256]{1,0:T(8,128)S(1)} %shard_map.79.p0), channel_id=1, source_target_pairs={{0,3},{1,0},{2,1},{3,2},{4,7},{5,4},{6,5},{7,6},{8,11},{9,8},{10,9... | collective-permute-start | bytes 24584 | tf_op jit(solution)/shard_map/ppermute | solution.py:348
  51.9 3.7 %collective-permute-start.4 = (f32[8,256]{1,0:T(8,128)S(1)}, f32[8,256]{1,0:T(8,128)S(1)}, u32[]{:S(2)}, u32[]{:S(2)}) collective-permute-start(f32[8,256]{1,0:T(8,128)S(1)} %shard_map.79.p0), channel_id=1, source_target_pairs={{0,1},{1,2},{2,3},{3,0},{4,5},{5,6},{6,7},{7,4},{8,9},{9,10},{10,1... | collective-permute-start | bytes 24584 | tf_op jit(solution)/shard_map/ppermute | solution.py:348
  57.5 9.8 %collective-permute-start.7 = (f32[8,256]{1,0:T(8,128)S(1)}, f32[8,256]{1,0:T(8,128)S(1)}, u32[]{:S(2)}, u32[]{:S(2)}) collective-permute-start(f32[8,256]{1,0:T(8,128)S(1)} %shard_map.80), channel_id=1, source_target_pairs={{0,4},{4,0},{1,5},{5,1},{2,6},{6,2},{3,7},{7,3},{8,12},{12,8},{9,1... | collective-permute-start | bytes 24584 | tf_op jit(solution)/shard_map/ppermute | solution.py:348
  68.1 14.1 %all-to-all-start.1 = ((f32[32,8,256]{2,1,0:T(8,128)}), f32[32,8,256]{2,1,0:T(8,128)S(1)}, u32[]{:S(2)}, u32[]{:S(2)}) async-start(f32[32,8,256]{2,1,0:T(8,128)} %broadcast_in_dim.7), calls=%async_computation.1 | async-start | bytes 524288 | tf_op jit(solution)/shard_map/all_to_all | solution.py:359
  85.1 4.1 %collective-permute-start.10 = (f32[8,256]{1,0:T(8,128)S(1)}, f32[8,256]{1,0:T(8,128)S(1)}, u32[]{:S(2)}, u32[]{:S(2)}) collective-permute-start(f32[8,256]{1,0:T(8,128)S(1)} %shard_map.81.p0), channel_id=1, source_target_pairs={{0,2},{1,3},{2,0},{3,1},{4,6},{5,7},{6,4},{7,5},{8,10},{9,11},{10,... | collective-permute-start | bytes 24584 | tf_op jit(solution)/shard_map/ppermute | solution.py:348
  85.6 3.6 %collective-permute-start.9 = (f32[8,256]{1,0:T(8,128)S(1)}, f32[8,256]{1,0:T(8,128)S(1)}, u32[]{:S(2)}, u32[]{:S(2)}) collective-permute-start(f32[8,256]{1,0:T(8,128)S(1)} %shard_map.81.p0), channel_id=1, source_target_pairs={{0,3},{1,0},{2,1},{3,2},{4,7},{5,4},{6,5},{7,6},{8,11},{9,8},{10,9... | collective-permute-start | bytes 24584 | tf_op jit(solution)/shard_map/ppermute | solution.py:348
  86.0 3.7 %collective-permute-start.8 = (f32[8,256]{1,0:T(8,128)S(1)}, f32[8,256]{1,0:T(8,128)S(1)}, u32[]{:S(2)}, u32[]{:S(2)}) collective-permute-start(f32[8,256]{1,0:T(8,128)S(1)} %shard_map.81.p0), channel_id=1, source_target_pairs={{0,1},{1,2},{2,3},{3,0},{4,5},{5,6},{6,7},{7,4},{8,9},{9,10},{10,1... | collective-permute-start | bytes 24584 | tf_op jit(solution)/shard_map/ppermute | solution.py:348
  95.2 35.9 %collective-permute-start.18 = (f32[4,8,32,512]{3,2,1,0:T(8,128)}, f32[4,8,32,512]{3,2,1,0:T(8,128)S(1)}, u32[]{:S(2)}, u32[]{:S(2)}) collective-permute-start(f32[4,8,32,512]{3,2,1,0:T(8,128)} %get-tuple-element.37), channel_id=1, source_target_pairs={{0,4},{4,0},{1,5},{5,1},{2,6},{6,2},{3,7},{7,3},{8,12},{12,8},{9,1... | collective-permute-start | bytes 6291464 | tf_op jit(solution)/shard_map/ppermute | solution.py:348
  109.5 4.0 %collective-permute-start.11 = (f32[8,256]{1,0:T(8,128)S(1)}, f32[8,256]{1,0:T(8,128)S(1)}, u32[]{:S(2)}, u32[]{:S(2)}) collective-permute-start(f32[8,256]{1,0:T(8,128)S(1)} %get-tuple-element.26.mine), channel_id=1, source_target_pairs={{0,4},{4,0},{1,5},{5,1},{2,6},{6,2},{3,7},{7,3},{8,12},{12,8},{9,1... | collective-permute-start | bytes 24584 | tf_op jit(solution)/shard_map/ppermute | solution.py:348
  133.0 8.5 %collective-permute-start.19 = (f32[4,32,512]{2,1,0:T(8,128)S(1)}, f32[4,32,512]{2,1,0:T(8,128)S(1)}, u32[]{:S(2)}, u32[]{:S(2)}) collective-permute-start(f32[4,32,512]{2,1,0:T(8,128)S(1)} %get-tuple-element.40), channel_id=1, source_target_pairs={{0,64},{64,128},{128,192},{192,0},{1,65},{65,129},{129,193},{193,1... | collective-permute-start | bytes 786440 | tf_op jit(solution)/shard_map/ppermute | solution.py:348
  138.2 5.4 %collective-permute-start.23 = (f32[4,32,512]{2,1,0:T(8,128)S(1)}, f32[4,32,512]{2,1,0:T(8,128)S(1)}, u32[]{:S(2)}, u32[]{:S(2)}) collective-permute-start(f32[4,32,512]{2,1,0:T(8,128)S(1)} %get-tuple-element.45), channel_id=1, source_target_pairs={{0,192},{64,0},{128,64},{192,128},{1,193},{65,1},{129,65},{193,129... | collective-permute-start | bytes 786440 | tf_op jit(solution)/shard_map/ppermute | solution.py:348
  138.2 9.7 %collective-permute-start.21 = (f32[4,32,512]{2,1,0:T(8,128)S(1)}, f32[4,32,512]{2,1,0:T(8,128)S(1)}, u32[]{:S(2)}, u32[]{:S(2)}) collective-permute-start(f32[4,32,512]{2,1,0:T(8,128)S(1)} %get-tuple-element.41), channel_id=1, source_target_pairs={{0,192},{64,0},{128,64},{192,128},{1,193},{65,1},{129,65},{193,129... | collective-permute-start | bytes 786440 | tf_op jit(solution)/shard_map/ppermute | solution.py:348
  141.5 9.4 %collective-permute-start.20 = (f32[4,32,512]{2,1,0:T(8,128)S(1)}, f32[4,32,512]{2,1,0:T(8,128)S(1)}, u32[]{:S(2)}, u32[]{:S(2)}) collective-permute-start(f32[4,32,512]{2,1,0:T(8,128)S(1)} %add.57), channel_id=1, source_target_pairs={{0,64},{64,128},{128,192},{192,0},{1,65},{65,129},{129,193},{193,1... | collective-permute-start | bytes 786440 | tf_op jit(solution)/shard_map/ppermute | solution.py:348
  143.5 10.1 %collective-permute-start.22 = (f32[4,32,512]{2,1,0:T(8,128)S(1)}, f32[4,32,512]{2,1,0:T(8,128)S(1)}, u32[]{:S(2)}, u32[]{:S(2)}) collective-permute-start(f32[4,32,512]{2,1,0:T(8,128)S(1)} %get-tuple-element.43), channel_id=1, source_target_pairs={{0,64},{64,128},{128,192},{192,0},{1,65},{65,129},{129,193},{193,1... | collective-permute-start | bytes 786440 | tf_op jit(solution)/shard_map/ppermute | solution.py:348
  143.7 10.0 %collective-permute-start.24 = (f32[4,32,512]{2,1,0:T(8,128)S(1)}, f32[4,32,512]{2,1,0:T(8,128)S(1)}, u32[]{:S(2)}, u32[]{:S(2)}) collective-permute-start(f32[4,32,512]{2,1,0:T(8,128)S(1)} %add.61), channel_id=1, source_target_pairs={{0,192},{64,0},{128,64},{192,128},{1,193},{65,1},{129,65},{193,129... | collective-permute-start | bytes 786440 | tf_op jit(solution)/shard_map/ppermute | solution.py:348
  146.3 24.3 %collective-permute-start.12 = (f32[264,512]{1,0:T(8,128)S(1)}, f32[264,512]{1,0:T(8,128)}, u32[]{:S(2)}, u32[]{:S(2)}) collective-permute-start(f32[264,512]{1,0:T(8,128)S(1)} %get-tuple-element.30.after), channel_id=1, source_target_pairs={{0,1},{1,2},{2,3},{3,0},{4,5},{5,6},{6,7},{7,4},{8,9},{9,10},{10,1... | collective-permute-start | bytes 1622024 | tf_op jit(solution)/shard_map/ppermute | solution.py:348
  147.9 18.6 %collective-permute-start.16 = (f32[264,512]{1,0:T(8,128)}, f32[264,512]{1,0:T(8,128)}, u32[]{:S(2)}, u32[]{:S(2)}) collective-permute-start(f32[264,512]{1,0:T(8,128)} %get-tuple-element.35), channel_id=1, source_target_pairs={{0,3},{1,0},{2,1},{3,2},{4,7},{5,4},{6,5},{7,6},{8,11},{9,8},{10,9... | collective-permute-start | bytes 1622024 | tf_op jit(solution)/shard_map/ppermute | solution.py:348
  154.6 39.0 %all-to-all-start.3 = ((f32[8,32,512]{2,1,0:T(8,128)}), f32[8,32,512]{2,1,0:T(8,128)}, u32[]{:S(2)}, u32[]{:S(2)}) async-start(f32[8,32,512]{2,1,0:T(8,128)} %pad_maximum_fusion.1), calls=%async_computation.3 | async-start | bytes 1048576 | tf_op jit(solution)/shard_map/all_to_all | solution.py:464
  166.4 13.9 %collective-permute-start.15 = (f32[264,512]{1,0:T(8,128)S(1)}, f32[264,512]{1,0:T(8,128)S(1)}, u32[]{:S(2)}, u32[]{:S(2)}) collective-permute-start(f32[264,512]{1,0:T(8,128)S(1)} %get-tuple-element.33), channel_id=1, source_target_pairs={{0,1},{1,2},{2,3},{3,0},{4,5},{5,6},{6,7},{7,4},{8,9},{9,10},{10,1... | collective-permute-start | bytes 1622024 | tf_op jit(solution)/shard_map/ppermute | solution.py:348
  167.8 13.0 %collective-permute-start.17 = (f32[264,512]{1,0:T(8,128)S(1)}, f32[264,512]{1,0:T(8,128)S(1)}, u32[]{:S(2)}, u32[]{:S(2)}) collective-permute-start(f32[264,512]{1,0:T(8,128)S(1)} %add.56), channel_id=1, source_target_pairs={{0,3},{1,0},{2,1},{3,2},{4,7},{5,4},{6,5},{7,6},{8,11},{9,8},{10,9... | collective-permute-start | bytes 1622024 | tf_op jit(solution)/shard_map/ppermute | solution.py:348
  170.5 21.8 %collective-permute-start.14 = (f32[264,512]{1,0:T(8,128)S(1)}, f32[264,512]{1,0:T(8,128)S(1)}, u32[]{:S(2)}, u32[]{:S(2)}) collective-permute-start(f32[264,512]{1,0:T(8,128)S(1)} %get-tuple-element.31), channel_id=1, source_target_pairs={{0,3},{1,0},{2,1},{3,2},{4,7},{5,4},{6,5},{7,6},{8,11},{9,8},{10,9... | collective-permute-start | bytes 1622024 | tf_op jit(solution)/shard_map/ppermute | solution.py:348
  171.7 20.6 %collective-permute-start.13 = (f32[264,512]{1,0:T(8,128)S(1)}, f32[264,512]{1,0:T(8,128)S(1)}, u32[]{:S(2)}, u32[]{:S(2)}) collective-permute-start(f32[264,512]{1,0:T(8,128)S(1)} %add.55), channel_id=1, source_target_pairs={{0,1},{1,2},{2,3},{3,0},{4,5},{5,6},{6,7},{7,4},{8,9},{9,10},{10,1... | collective-permute-start | bytes 1622024 | tf_op jit(solution)/shard_map/ppermute | solution.py:348
where the time goes:
time: 199 us; the launch traced here: 195 us
  starting transfers between devices  84.2 us (42%)
  waiting for transfers between devices  61.2 us (31%)
  Pallas kernels  27 us (14%)
  blocking collectives  12.7 us (6%)
  other arithmetic  7.1 us (4%)
    ppermute x25, starting transfers between devices, shift(): return lax.ppermute(a, axis, [(i, (i + by) % size) for i in range(size)])  59.4 us
    ppermute x25, waiting for transfers between devices, shift(): return lax.ppermute(a, axis, [(i, (i + by) % size) for i in range(size)])  40.9 us
    pallas_call x10, Pallas kernels, call(): pl.pallas_call(kernel, out_shape=outs, in_specs=specs, out_specs=out_spec...  27 us
    all_to_all x2, waiting for transfers between devices, over_src(): return (lax.all_to_all(copies, ('y', 'z'), 0, 0, tiled=True), other)  20.3 us
    all_to_all x2, starting transfers between devices, over_src(): return (lax.all_to_all(copies, ('y', 'z'), 0, 0, tiled=True), other)  13 us
    all_to_all x1, blocking collectives, over_src(): return (lax.all_to_all(copies, ('y', 'z'), 0, 0, tiled=True), other)  12.7 us
    all_to_all x1, starting transfers between devices, program(): got = lax.all_to_all(summed, 'z', 0, 0, tiled=True)  11.9 us
  transfers between devices with their start and end apart: 28, of which 19 were waited for; matrix products, arithmetic and copies ran while one was open for 2% of the time, Pallas kernels for 3%

commit v1 on v0

v1 whole, which is shorter than its diff:
```python
import functools

import jax
import jax.numpy as jnp
from jax import lax
from jax.experimental import pallas as pl
from jax.experimental.pallas import tpu as pltpu
from jax.sharding import Mesh, PartitionSpec as P


BLK = 256
ITERS = 3
NB = 8
CAP = 16
D = 512
NX, NY, NZ, NC = 4, 4, 8, 2
FLOOR = -1e30
INV_TEMP = 0.15
STEP = 64


VMEM = pl.BlockSpec(memory_space=pltpu.VMEM)
SMEM = pl.BlockSpec(memory_space=pltpu.SMEM)
HBM = pl.BlockSpec(memory_space=pltpu.HBM)
f32 = jnp.float32


def lse_of(parts):
    peak = functools.reduce(jnp.maximum, parts)
    total = sum(jnp.exp(p - peak) for p in parts)
    return peak + jnp.log(total)


def lse_stack(ref):
    peak = jnp.max(ref[...], axis=0)
    total = jnp.sum(jnp.exp(ref[...] - peak[None]), axis=0)
    return peak + jnp.log(total)


def slots(cnt, pairs, body):
    def step(k, _):
        pair = pairs[k]
        body(k, pair // NB, pair % NB)
        return 0

    lax.fori_loop(0, cnt[0], step, 0)


def every_slot(cnt, act):
    def step(k, _):
        act(k)
        return 0

    lax.fori_loop(0, cnt[0], step, 0)


def fetch_scores(cnt, held, scores, sem):
    every_slot(cnt, lambda k: pltpu.make_async_copy(held.at[k], scores.at[k], sem.at[k]).start())
    return lambda k: pltpu.make_async_copy(held.at[k], scores.at[k], sem.at[k]).wait()


def fetch_blocks(held, out, sem):
    copies = [
        pltpu.make_async_copy(held.at[pl.ds(i * BLK, BLK), :], out.at[i], sem.at[i])
        for i in range(NB)
    ]
    for copy in copies:
        copy.start()
    return copies


def to_columns(rows):
    padded = jnp.concatenate([rows, jnp.zeros((120, BLK), f32)], axis=0)
    return jnp.transpose(padded)


def spread_columns(rows, out):
    cols = to_columns(rows)
    for a in range(NB):
        out[a] = jnp.broadcast_to(cols[:, a : a + 1], (BLK, 128))


def columns_to_rows(columns):
    lane = lax.broadcasted_iota(jnp.int32, (BLK, 128), 1)
    table = jnp.zeros((BLK, 128), f32)
    for a, column in enumerate(columns):
        table = jnp.where(lane == a, column, table)
    return jnp.transpose(table)[:NB]


def row_totals(cnt, pairs, scores, v, m_ref, s_ref, lse_out):
    s_ref[...] = jnp.zeros(s_ref.shape, f32)

    def body(k, a, b):
        shift = v[pl.ds(b, 1), :] if v is not None else None
        for r in range(0, BLK, STEP):
            rows = slice(r, r + STEP)
            tile = scores[k, rows, :]
            if shift is not None:
                tile = tile + shift
            peak = m_ref[a, rows, :]
            s_ref[a, rows, :] += jnp.exp(tile[:, :128] - peak) + jnp.exp(tile[:, 128:] - peak)

    slots(cnt, pairs, body)
    for a in range(NB):
        for h in range(0, BLK, 128):
            rows = slice(h, h + 128)
            peaks = jnp.transpose(m_ref[a, rows, :])
            totals = jnp.transpose(s_ref[a, rows, :])
            peak = jnp.max(peaks, axis=0, keepdims=True)
            total = jnp.sum(totals * jnp.exp(peaks - peak), axis=0, keepdims=True)
            lse_out[a : a + 1, rows] = jnp.where(total > 0, peak + jnp.log(total), FLOOR)


def first_kernel(
    cnt, pairs, text, image, held, lse_out, m_ref, s_ref, scores, texts, images, sem, tsem, isem
):
    copies = fetch_blocks(text, texts, tsem) + fetch_blocks(image, images, isem)
    m_ref[...] = jnp.full(m_ref.shape, FLOOR, f32)
    for copy in copies:
        copy.wait()

    last = cnt[0] - 1

    def two(i, _):
        picks = []
        for k in (2 * i, jnp.minimum(2 * i + 1, last)):
            pair = pairs[k]
            a, b = pair // NB, pair % NB
            tile = lax.dot_general(
                texts[a], images[b], (((1,), (1,)), ((), ())), preferred_element_type=f32
            )
            picks.append((k, a, tile * INV_TEMP))
        for k, a, tile in picks:
            scores[k] = tile
            m_ref[a] = jnp.maximum(m_ref[a], jnp.maximum(tile[:, :128], tile[:, 128:]))
        return 0

    lax.fori_loop(0, (cnt[0] + 1) // 2, two, 0)
    every_slot(cnt, lambda k: pltpu.make_async_copy(scores.at[k], held.at[k], sem.at[k]).start())
    row_totals(cnt, pairs, scores, None, m_ref, s_ref, lse_out)
    every_slot(cnt, lambda k: pltpu.make_async_copy(scores.at[k], held.at[k], sem.at[k]).wait())


def row_sums(cnt, pairs, tile_of, s_ref, out):
    s_ref[...] = jnp.zeros(s_ref.shape, f32)

    def body(k, a, b):
        for r in range(0, BLK, STEP):
            rows = slice(r, r + STEP)
            tile = tile_of(k, a, b, rows)
            s_ref[a, rows, :] += tile[:, :128] + tile[:, 128:]

    slots(cnt, pairs, body)
    for a in range(NB):
        for h in range(0, BLK, 128):
            rows = slice(h, h + 128)
            out[a : a + 1, rows] = jnp.sum(jnp.transpose(s_ref[a, rows, :]), axis=0, keepdims=True)


def plan_kernel(
    cnt, pairs, held, parts, mass, u, plan, out, v_ref, u_ref, s_ref, scores, sem, out_sem
):
    arrive = fetch_scores(cnt, held, scores, sem)
    v_ref[...] = mass[...] - lse_stack(parts)
    spread_columns(u[...], u_ref)

    def tile_of(k, a, b, rows):
        if rows.start == 0:
            arrive(k)
        tile = scores[k, rows, :] + v_ref[pl.ds(b, 1), :]
        shift = u_ref[a, rows, :]
        tile = jnp.exp(tile + jnp.concatenate([shift, shift], axis=1))
        scores[k, rows, :] = tile
        if rows.stop == BLK:
            pltpu.make_async_copy(scores.at[k], plan.at[k], out_sem.at[k]).start()
        return tile

    row_sums(cnt, pairs, tile_of, s_ref, out)
    every_slot(cnt, lambda k: pltpu.make_async_copy(scores.at[k], plan.at[k], out_sem.at[k]).wait())


def row_kernel(cnt, pairs, held, parts, mass, out, b_ref, s_ref, plan, sem):
    arrive = fetch_scores(cnt, held, plan, sem)
    b_ref[...] = jnp.exp(mass[...]) / jnp.sum(parts[...], axis=0)

    def tile_of(k, a, b, rows):
        if rows.start == 0:
            arrive(k)
        return plan[k, rows, :] * b_ref[pl.ds(b, 1), :]

    row_sums(cnt, pairs, tile_of, s_ref, out)


def col_peaks(cnt, pairs, scores, arrive, u, u_ref, m_ref, s_ref):
    spread_columns(u, u_ref)
    m_ref[...] = jnp.full(m_ref.shape, FLOOR, f32)
    s_ref[...] = jnp.zeros(s_ref.shape, f32)

    def peaks(k, a, b):
        arrive(k)
        for half in range(2):
            lanes = slice(half * 128, half * 128 + 128)
            best = m_ref[b, :, lanes]
            for r in range(0, BLK, STEP):
                tile = scores[k, r : r + STEP, lanes] + u_ref[a, r : r + STEP, :]
                best = jnp.maximum(best, jnp.max(tile.reshape(STEP // 8, 8, 128), axis=0))
            m_ref[b, :, lanes] = best

    slots(cnt, pairs, peaks)
    for b in range(NB):
        m_ref[b] = jnp.broadcast_to(jnp.max(m_ref[b], axis=0, keepdims=True), (8, BLK))


def col_lse(m_ref, s_ref, lse_out):
    for b in range(NB):
        total = jnp.sum(s_ref[b], axis=0, keepdims=True)
        lse_out[b : b + 1, :] = jnp.where(total > 0, m_ref[b, :1, :] + jnp.log(total), FLOOR)


def col_kernel(
    cnt, pairs, held, p0, p1, p2, p3, mass, lse_out, u_out, u_ref, m_ref, s_ref, scores, sem
):
    arrive = fetch_scores(cnt, held, scores, sem)
    u = mass[...] - lse_of([p0[...], p1[...], p2[...], p3[...]])
    u_out[...] = u
    col_peaks(cnt, pairs, scores, arrive, u, u_ref, m_ref, s_ref)

    def totals(k, a, b):
        for half in range(2):
            lanes = slice(half * 128, half * 128 + 128)
            peak = m_ref[b, :, lanes]
            total = s_ref[b, :, lanes]
            for r in range(0, BLK, STEP):
                tile = scores[k, r : r + STEP, lanes] + u_ref[a, r : r + STEP, :]
                tile = jnp.exp(tile.reshape(STEP // 8, 8, 128) - peak[None])
                total = total + jnp.sum(tile, axis=0)
            s_ref[b, :, lanes] = total

    slots(cnt, pairs, totals)
    col_lse(m_ref, s_ref, lse_out)


def col_sum_kernel(cnt, pairs, held, p0, p1, p2, p3, mass, out, a_ref, s_ref, plan, sem):
    arrive = fetch_scores(cnt, held, plan, sem)
    spread_columns(jnp.exp(mass[...]) / (p0[...] + p1[...] + p2[...] + p3[...]), a_ref)
    s_ref[...] = jnp.zeros(s_ref.shape, f32)

    def body(k, a, b):
        arrive(k)
        for half in range(2):
            lanes = slice(half * 128, half * 128 + 128)
            total = s_ref[b, :, lanes]
            for r in range(0, BLK, STEP):
                tile = plan[k, r : r + STEP, lanes] * a_ref[a, r : r + STEP, :]
                total = total + jnp.sum(tile.reshape(STEP // 8, 8, 128), axis=0)
            s_ref[b, :, lanes] = total

    slots(cnt, pairs, body)
    for b in range(NB):
        out[b : b + 1, :] = jnp.sum(s_ref[b], axis=0, keepdims=True)


def last_col_kernel(
    cnt, pairs, place, held, p0, p1, p2, p3, mass, text, out, a_out, keep, send,
    a_ref, s_ref, plan, sem, texts, tsem, w_ref, acc,
):
    arrive = fetch_scores(cnt, held, plan, sem)
    copies = fetch_blocks(text, texts, tsem)
    scale = jnp.exp(mass[...]) / (p0[...] + p1[...] + p2[...] + p3[...])
    a_out[...] = scale
    spread_columns(scale, a_ref)
    s_ref[...] = jnp.zeros(s_ref.shape, f32)
    acc[...] = jnp.zeros(acc.shape, f32)
    for copy in copies:
        copy.wait()

    def body(k, a, b):
        arrive(k)
        for half in range(2):
            lanes = slice(half * 128, half * 128 + 128)
            total = s_ref[b, :, lanes]
            for r in range(0, BLK, STEP):
                tile = plan[k, r : r + STEP, lanes] * a_ref[a, r : r + STEP, :]
                total = total + jnp.sum(tile.reshape(STEP // 8, 8, 128), axis=0)
                w_ref[r : r + STEP, lanes] = tile.astype(jnp.bfloat16)
            s_ref[b, :, lanes] = total
        acc[b] += lax.dot_general(
            w_ref[...], texts[a], (((0,), (0,)), ((), ())), preferred_element_type=f32
        )

    slots(cnt, pairs, body)
    for b in range(NB):
        out[b : b + 1, :] = jnp.sum(s_ref[b], axis=0, keepdims=True)
    y, c = place[1], place[2]
    for r in range(NY):
        b0 = 2 * lax.rem(y + r, NY)
        for z in range(NZ):
            b = b0 + z // 4
            for dst, core in ((keep, c), (send, 1 - c)):
                dst[r, z] = acc[b, pl.ds(pl.multiple_of((z % 4) * 64 + core * 32, 32), 32), :]


def add_kernel(keep, got, *outs):
    for r in range(NY):
        for h in range(2):
            outs[2 * r + h][...] = keep[r, 4 * h : 4 * h + 4] + got[r, 4 * h : 4 * h + 4]


def tgt_norm_kernel(place, parts, stack, out, c_ref):
    y, c, z = place[1], place[2], place[3]
    b = 2 * y + z // 4
    lane = lax.broadcasted_iota(jnp.int32, (BLK, 128), 1)
    cols = to_columns(jnp.sum(stack[...], axis=0))
    c_ref[...] = jnp.where(lane == b, cols, 0.0)
    rows = pl.ds(pl.multiple_of(lax.rem(z, 4) * 64 + c * 32, 32), 32)
    mass = jnp.sum(c_ref[rows, :], axis=1, keepdims=True)
    out[...] = jnp.sum(parts[...], axis=0) / mass


def final_kernel(offset, cnt, pairs, place, held, parts, mass, scale, image, *refs):
    src_out = refs[:4]
    scores, sem, images, isem, b_ref, a_ref, w_ref, acc, rsum = refs[4:]
    start = 2 * place[0] + offset

    def mine(act):
        def step(k, _):
            pair = pairs[k]
            a = pair // NB
            q = lax.rem(a + 2 * NB - start, NB)

            @pl.when(q < 4)
            def _():
                act(k, q, a, pair % NB)

            return 0

        lax.fori_loop(0, cnt[0], step, 0)

    mine(lambda k, q, a, b: pltpu.make_async_copy(held.at[k], scores.at[k], sem.at[k]).start())
    copies = fetch_blocks(image, images, isem)
    b_ref[...] = jnp.exp(mass[...]) / jnp.sum(parts[...], axis=0)
    spread_columns(scale[...], a_ref)
    acc[...] = jnp.zeros(acc.shape, f32)
    rsum[...] = jnp.zeros(rsum.shape, f32)
    for copy in copies:
        copy.wait()

    def body(k, q, a, b):
        pltpu.make_async_copy(held.at[k], scores.at[k], sem.at[k]).wait()
        v = b_ref[pl.ds(b, 1), :]
        for r in range(0, BLK, STEP):
            rows = slice(r, r + STEP)
            for half in range(2):
                lanes = slice(half * 128, half * 128 + 128)
                plan = scores[k, rows, lanes] * a_ref[a, rows, :] * v[:, lanes]
                rsum[q, rows, :] += plan
                w_ref[rows, lanes] = plan.astype(jnp.bfloat16)
        acc[q] += jnp.dot(w_ref[...], images[b], preferred_element_type=f32)

    mine(body)
    masses = columns_to_rows([jnp.sum(rsum[q], axis=1, keepdims=True) for q in range(4)])
    for q in range(4):
        src_out[q][:BLK, :] = acc[q]
        src_out[q][BLK:, :BLK] = jnp.broadcast_to(masses[q : q + 1, :], (8, BLK))
        src_out[q][BLK:, BLK:] = jnp.zeros((8, D - BLK), f32)


def src_norm_kernel(*refs):
    out = refs[-1]
    for h in range(2):
        own, plus, minus = refs[3 * h : 3 * h + 3]
        rows = slice(BLK, BLK + 8)
        mass = own[rows, :BLK] + plus[rows, :BLK] + minus[rows, :BLK]
        scale = to_columns(1.0 / mass)[:, :1]
        out[h * BLK : h * BLK + BLK, :] = (
            own[:BLK, :] + plus[:BLK, :] + minus[:BLK, :]
        ) * scale


def call(kernel, outs, args, smem, scratch=(), mib=50, hbm=(), flops=1 << 24):
    n = len(args)
    specs = [SMEM if i < smem else HBM if i in hbm else VMEM for i in range(n)]
    flat, tree = jax.tree.flatten(outs)
    out_specs = tree.unflatten([HBM if n + i in hbm else VMEM for i in range(len(flat))])
    return pl.pallas_call(
        kernel,
        out_shape=outs,
        in_specs=specs,
        out_specs=out_specs,
        scratch_shapes=list(scratch),
        compiler_params=pltpu.CompilerParams(vmem_limit_bytes=mib << 20),
        cost_estimate=pl.CostEstimate(
            flops=flops, bytes_accessed=8 << 20, transcendentals=CAP * BLK * BLK
        ),
    )(*args)


def sds(*shape):
    return jax.ShapeDtypeStruct(shape, f32)


def shift(a, axis, size, by):
    return lax.ppermute(a, axis, [(i, (i + by) % size) for i in range(size)])


def over_x(part):
    return [part] + [shift(part, "x", NX, k) for k in (1, 3, 2)]


def over_src(part, join):
    other = shift(part, "c", NC, 1)
    both = join([part, other])
    copies = jnp.broadcast_to(both[None], (NY * NZ, NB, BLK))
    return lax.all_to_all(copies, ("y", "z"), 0, 0, tiled=True)


def ring_scatter(own_a, own_b, plus_a, plus_b, far_a, far_b, minus_a, minus_b, axis, size):
    def move(value, by):
        return shift(value, axis, size, by)

    relay_up = move(far_a, 1)
    relay_down = move(far_b, -1)
    from_below_b = move(plus_b, 1)
    from_above_a = move(minus_a, -1)
    from_below_a = move(plus_a + relay_up, 1)
    from_above_b = move(minus_b + relay_down, -1)
    return (own_a, from_below_a, from_above_a), (own_b, from_below_b, from_above_b)


def program(text, image, log_mass_src, log_mass_tgt, pairs, count):
    mass_src = log_mass_src.reshape(NB, BLK)
    mass_tgt = log_mass_tgt.reshape(NB, BLK)
    pairs = pairs[:, 0] * NB + pairs[:, 1]
    place = jnp.stack([lax.axis_index(name) for name in ("x", "y", "c", "z")])
    row_scratch = [pltpu.VMEM((NB, BLK, 128), f32)] * 2
    col_scratch = [pltpu.VMEM((NB, BLK, 128), f32)] + [pltpu.VMEM((NB, 8, BLK), f32)] * 2
    tiles = [pltpu.VMEM((CAP, BLK, BLK), f32), pltpu.SemaphoreType.DMA((CAP,))]
    blocks = [pltpu.VMEM((NB, BLK, D), jnp.bfloat16)]
    block_sem = [pltpu.SemaphoreType.DMA((NB,))]
    stats = sds(NB, BLK)
    scores, part = call(
        first_kernel,
        (sds(CAP, BLK, BLK), stats),
        (count, pairs, text, image),
        2,
        row_scratch + tiles[:1] + blocks * 2 + tiles[1:] + block_sem * 2,
        52,
        (2, 3, 4),
        1 << 30,
    )
    part, u = call(
        col_kernel,
        (stats, stats),
        (count, pairs, scores, *over_x(part), mass_src),
        2,
        col_scratch + tiles,
        hbm=(2,),
    )
    stack = over_src(part, lse_of)
    plan, part = call(
        plan_kernel,
        (sds(CAP, BLK, BLK), stats),
        (count, pairs, scores, stack, mass_tgt, u),
        2,
        [pltpu.VMEM((NB, BLK), f32)] + row_scratch + tiles + tiles[1:],
        hbm=(2, 6),
    )
    for _ in range(ITERS - 2):
        part = call(
            col_sum_kernel,
            stats,
            (count, pairs, plan, *over_x(part), mass_src),
            2,
            [col_scratch[0], col_scratch[1]] + tiles,
            hbm=(2,),
        )
        stack = over_src(part, sum)
        part = call(
            row_kernel,
            stats,
            (count, pairs, plan, stack, mass_tgt),
            2,
            [pltpu.VMEM((NB, BLK), f32), row_scratch[0]] + tiles,
            hbm=(2,),
        )
    half = sds(NY, NZ, 32, D)
    part, scale, keep, send = call(
        last_col_kernel,
        (stats, stats, half, half),
        (count, pairs, place, plan, *over_x(part), mass_src, text),
        3,
        [col_scratch[0], col_scratch[1]]
        + tiles
        + blocks
        + block_sem
        + [pltpu.VMEM((BLK, BLK), jnp.bfloat16), pltpu.VMEM((NB, BLK, D), f32)],
        50,
        (3, 9),
        1 << 31,
    )
    got = shift(send, "c", NC, 1)
    stack = over_src(part, sum)
    halves = call(add_kernel, tuple([sds(4, 32, D)] * 8), (keep, got), 0, (), 16)

    def final(offset):
        return call(
            functools.partial(final_kernel, offset),
            tuple([sds(BLK + 8, D)] * 4),
            (count, pairs, place, plan, stack, mass_tgt, scale, image),
            3,
            tiles
            + blocks
            + block_sem
            + [
                pltpu.VMEM((NB, BLK), f32),
                pltpu.VMEM((NB, BLK, 128), f32),
                pltpu.VMEM((BLK, BLK), jnp.bfloat16),
                pltpu.VMEM((4, BLK, D), f32),
                pltpu.VMEM((4, BLK, 128), f32),
            ],
            50,
            (3, 7),
            1 << 29,
        )

    far = final(3)
    near = final(7)
    part_a, part_b = ring_scatter(*near[1:], *far, near[0], "x", NX)
    tgt_a, tgt_b = ring_scatter(*halves, "y", NY)
    summed = jnp.concatenate([sum(tgt_a), sum(tgt_b)], axis=0)
    got = lax.all_to_all(summed, "z", 0, 0, tiled=True)
    tgt_map = call(
        tgt_norm_kernel, sds(32, D), (place, got, stack), 1, [pltpu.VMEM((BLK, 128), f32)], 16
    )
    src_map = call(src_norm_kernel, sds(2 * BLK, D), (*part_a, *part_b), 0, (), 16)
    return (src_map, tgt_map)


def solution(mesh):
    grid = Mesh(mesh.devices.reshape(NY, NZ, NC, NX), ("y", "z", "c", "x"))
    src = ("y", "z", "c")
    return jax.shard_map(
        program,
        mesh=grid,
        in_specs=(P(src, None), P("x", None), P(src), P("x"), P((*src, "x"), None), P((*src, "x"))),
        out_specs=(P((*src, "x"), None), P(("x", *src), None)),
        check_vma=False,
    )
```

time: 199 us -> 178 us (0.89)
  blocking collectives: 12.7 us -> 0 us
  waiting for transfers between devices: 61.2 us -> 54.1 us
  Pallas kernels: 27 us -> 30.2 us
  starting transfers between devices: 84.2 us -> 81.9 us
    all_to_all x1 -> x0, blocking collectives: 12.7 us -> none  [over_src(): return (lax.all_to_all(copies, ('y', 'z'), 0, 0, tiled=True), other)]
    ppermute x25, waiting for transfers between devices: 40.9 us -> 33.8 us  [shift(): return lax.ppermute(a, axis, [(i, (i + by) % size) for i in range(size)])]
    all_to_all x1, starting transfers between devices: 11.9 us -> 5.71 us  [program(): got = lax.all_to_all(summed, 'z', 0, 0, tiled=True)]
    pallas_call x10 -> x11, Pallas kernels: 27 us -> 30.2 us  [call(): pl.pallas_call(kernel, out_shape=outs, in_specs=specs, out_specs=out_spec...]
    all_to_all x2 -> x3, starting transfers between devices: 13 us -> 15.5 us  [over_src(): return lax.all_to_all(copies, ('y', 'z'), 0, 0, tiled=True)]
    all_to_all x2 -> x3, waiting for transfers between devices: 20.3 us -> 20.3 us  [over_src(): return lax.all_to_all(copies, ('y', 'z'), 0, 0, tiled=True)]
  transfers between devices with their start and end apart: 28 -> 29, of which waited for: 19 -> 13; matrix products, arithmetic and copies ran while one was open for 2% -> 3% of each run, Pallas kernels for 3% -> 7%
where the time goes in v1:
time: 178 us; the launch traced here: 176 us
  starting transfers between devices  81.9 us (46%)
  waiting for transfers between devices  54.1 us (30%)
  Pallas kernels  30.2 us (17%)
  other arithmetic  6.13 us (3%)
  local copies, waits for them, and re-layouts  2.19 us (1%)
    ppermute x25, starting transfers between devices, shift(): return lax.ppermute(a, axis, [(i, (i + by) % size) for i in range(size)])  60.7 us
    ppermute x25, waiting for transfers between devices, shift(): return lax.ppermute(a, axis, [(i, (i + by) % size) for i in range(size)])  33.8 us
    pallas_call x11, Pallas kernels, call(): pl.pallas_call(kernel, out_shape=outs, in_specs=specs, out_specs=out_spec...  30.2 us
    all_to_all x3, waiting for transfers between devices, over_src(): return lax.all_to_all(copies, ('y', 'z'), 0, 0, tiled=True)  20.3 us
    all_to_all x3, starting transfers between devices, over_src(): return lax.all_to_all(copies, ('y', 'z'), 0, 0, tiled=True)  15.5 us
    all_to_all x1, starting transfers between devices, program(): got = lax.all_to_all(summed, 'z', 0, 0, tiled=True)  5.71 us
  transfers between devices with their start and end apart: 29, of which 13 were waited for; matrix products, arithmetic and copies ran while one was open for 3% of the time, Pallas kernels for 7%

profile of v1, /device:TPU:1, one launch (start us, length us, event | category | flops | bytes accessed | tf_op | source)
XLA Modules:
  0.0 176.1 jit_solution(9828928434490931031)
XLA Ops:
  2.1 4.1 %shard_map.77 = (f32[16,256,256]{2,1,0:T(8,128)}, f32[8,256]{1,0:T(8,128)S(1)}) custom-call(s32[1]{0:T(128)S(6)} %copy.8.cnt, s32[16]{0:T(128)S(1)} %add_bitcast_fusion.pairs, bf16[2048,512]{1,0:T(8,128)(2,1)} %text.3, bf16[2048,512]{1,0:T(8,128)(2,1)} %image.5), custom_call_target="tpu_custom_call" | custom-call | flops 1073741824 | bytes 8388608 | tf_op jit(solution)/shard_map/pallas_call | solution.py:386
  6.2 2.1 %collective-permute-start = (f32[8,256]{1,0:T(8,128)S(1)}, f32[8,256]{1,0:T(8,128)S(1)}, u32[]{:S(2)}, u32[]{:S(2)}) collective-permute-start(f32[8,256]{1,0:T(8,128)S(1)} %get-tuple-element.29.p0), channel_id=1, source_target_pairs={{0,1},{1,2},{2,3},{3,0},{4,5},{5,6},{6,7},{7,4},{8,9},{9,10},{10,1... | collective-permute-start | bytes 24584 | tf_op jit(solution)/shard_map/ppermute | solution.py:404
  8.3 3.4 %collective-permute-start.1 = (f32[8,256]{1,0:T(8,128)S(1)}, f32[8,256]{1,0:T(8,128)S(1)}, u32[]{:S(2)}, u32[]{:S(2)}) collective-permute-start(f32[8,256]{1,0:T(8,128)S(1)} %get-tuple-element.29.p0), channel_id=1, source_target_pairs={{0,3},{1,0},{2,1},{3,2},{4,7},{5,4},{6,5},{7,6},{8,11},{9,8},{10,9... | collective-permute-start | bytes 24584 | tf_op jit(solution)/shard_map/ppermute | solution.py:404
  11.8 1.6 collective-permute-start.2
  13.4 2.3 %collective-permute-done.2.p3 = f32[8,256]{1,0:T(8,128)S(1)} collective-permute-done((f32[8,256]{1,0:T(8,128)S(1)}, f32[8,256]{1,0:T(8,128)S(1)}, u32[]{:S(2)}, u32[]{:S(2)}) %collective-permute-start.2) | collective-permute-done | bytes 8224 | tf_op jit(solution)/shard_map/ppermute | solution.py:404
  15.8 1.9 %shard_map.78 = (f32[8,256]{1,0:T(8,128)S(1)}, f32[8,256]{1,0:T(8,128)S(1)}) custom-call(s32[1]{0:T(128)S(6)} %copy.8.cnt, s32[16]{0:T(128)S(1)} %add_bitcast_fusion.pairs, f32[16,256,256]{2,1,0:T(8,128)} %get-tuple-element.28.held, f32[8,256]{1,0:T(8,128)S(1)} %get-tuple-element.29.p0, f32[8,256]{1,0:T(8,128)S(1)} %collective-permute-done.p1, ...), custom_call_target="tpu_custom_call" | custom-call | flops 16777216 | bytes 8388608 | tf_op jit(solution)/shard_map/pallas_call | solution.py:386
  17.7 8.0 %collective-permute-start.3 = (f32[8,256]{1,0:T(8,128)S(1)}, f32[8,256]{1,0:T(8,128)S(1)}, u32[]{:S(2)}, u32[]{:S(2)}) collective-permute-start(f32[8,256]{1,0:T(8,128)S(1)} %get-tuple-element.30), channel_id=1, source_target_pairs={{0,4},{4,0},{1,5},{5,1},{2,6},{6,2},{3,7},{7,3},{8,12},{12,8},{9,1... | collective-permute-start | bytes 24584 | tf_op jit(solution)/shard_map/ppermute | solution.py:404
  27.3 7.8 %all-to-all-start = ((f32[32,8,256]{2,1,0:T(8,128)}), f32[32,8,256]{2,1,0:T(8,128)S(1)}, u32[]{:S(2)}, u32[]{:S(2)}) async-start(f32[32,8,256]{2,1,0:T(8,128)} %broadcast_in_dim.6), calls=%async_computation | async-start | bytes 524288 | tf_op jit(solution)/shard_map/all_to_all | solution.py:415
  35.1 10.1 %all-to-all-done.parts = f32[32,8,256]{2,1,0:T(8,128)S(1)} async-done(((f32[32,8,256]{2,1,0:T(8,128)}), f32[32,8,256]{2,1,0:T(8,128)S(1)}, u32[]{:S(2)}, u32[]{:S(2)}) %all-to-all-start) | async-done | bytes 262176 | tf_op jit(solution)/shard_map/all_to_all | solution.py:415
  45.2 2.6 %shard_map.79 = (f32[16,256,256]{2,1,0:T(8,128)}, f32[8,256]{1,0:T(8,128)S(1)}) custom-call(s32[1]{0:T(128)S(6)} %copy.8.cnt, s32[16]{0:T(128)S(1)} %add_bitcast_fusion.pairs, f32[16,256,256]{2,1,0:T(8,128)} %get-tuple-element.28.held, f32[32,8,256]{2,1,0:T(8,128)S(1)} %all-to-all-done.parts, f32[8,256]{1,0:T(8,128)S(1)} %reshape.17.mass, ...), custom_call_target="tpu_custom_call" | custom-call | flops 16777216 | bytes 8388608 | tf_op jit(solution)/shard_map/pallas_call | solution.py:386
  47.9 2.7 %collective-permute-start.5 = (f32[8,256]{1,0:T(8,128)S(1)}, f32[8,256]{1,0:T(8,128)S(1)}, u32[]{:S(2)}, u32[]{:S(2)}) collective-permute-start(f32[8,256]{1,0:T(8,128)S(1)} %get-tuple-element.33.p0), channel_id=1, source_target_pairs={{0,3},{1,0},{2,1},{3,2},{4,7},{5,4},{6,5},{7,6},{8,11},{9,8},{10,9... | collective-permute-start | bytes 24584 | tf_op jit(solution)/shard_map/ppermute | solution.py:404
  50.6 2.3 %collective-permute-start.6 = (f32[8,256]{1,0:T(8,128)S(1)}, f32[8,256]{1,0:T(8,128)S(1)}, u32[]{:S(2)}, u32[]{:S(2)}) collective-permute-start(f32[8,256]{1,0:T(8,128)S(1)} %get-tuple-element.33.p0), channel_id=1, source_target_pairs={{0,2},{1,3},{2,0},{3,1},{4,6},{5,7},{6,4},{7,5},{8,10},{9,11},{10,... | collective-permute-start | bytes 24584 | tf_op jit(solution)/shard_map/ppermute | solution.py:404
  52.8 1.7 collective-permute-done.6.p3
  54.6 1.8 %shard_map.80 = f32[8,256]{1,0:T(8,128)S(1)} custom-call(s32[1]{0:T(128)S(6)} %copy.8.cnt, s32[16]{0:T(128)S(1)} %add_bitcast_fusion.pairs, f32[16,256,256]{2,1,0:T(8,128)} %get-tuple-element.32.held, f32[8,256]{1,0:T(8,128)S(1)} %get-tuple-element.33.p0, f32[8,256]{1,0:T(8,128)S(1)} %collective-permute-done.4.p1, f32[8,256]{1,0:T(8,128)S(1)} %collective-permute-done.5.p2, ...), custom_call_target="tpu_custom_call" | custom-call | flops 16777216 | bytes 8388608 | tf_op jit(solution)/shard_map/pallas_call | solution.py:386
  56.3 7.7 %collective-permute-start.7 = (f32[8,256]{1,0:T(8,128)S(1)}, f32[8,256]{1,0:T(8,128)S(1)}, u32[]{:S(2)}, u32[]{:S(2)}) collective-permute-start(f32[8,256]{1,0:T(8,128)S(1)} %shard_map.80), channel_id=1, source_target_pairs={{0,4},{4,0},{1,5},{5,1},{2,6},{6,2},{3,7},{7,3},{8,12},{12,8},{9,1... | collective-permute-start | bytes 24584 | tf_op jit(solution)/shard_map/ppermute | solution.py:404
  65.6 3.9 %all-to-all-start.1 = ((f32[32,8,256]{2,1,0:T(8,128)}), f32[32,8,256]{2,1,0:T(8,128)S(1)}, u32[]{:S(2)}, u32[]{:S(2)}) async-start(f32[32,8,256]{2,1,0:T(8,128)} %broadcast_in_dim.7), calls=%async_computation.1 | async-start | bytes 524288 | tf_op jit(solution)/shard_map/all_to_all | solution.py:415
  69.5 10.3 %all-to-all-done.1.parts = f32[32,8,256]{2,1,0:T(8,128)S(1)} async-done(((f32[32,8,256]{2,1,0:T(8,128)}), f32[32,8,256]{2,1,0:T(8,128)S(1)}, u32[]{:S(2)}, u32[]{:S(2)}) %all-to-all-start.1) | async-done | bytes 262176 | tf_op jit(solution)/shard_map/all_to_all | solution.py:415
  79.8 2.1 %shard_map.81.p0 = f32[8,256]{1,0:T(8,128)S(1)} custom-call(s32[1]{0:T(128)S(6)} %copy.8.cnt, s32[16]{0:T(128)S(1)} %add_bitcast_fusion.pairs, f32[16,256,256]{2,1,0:T(8,128)} %get-tuple-element.32.held, f32[32,8,256]{2,1,0:T(8,128)S(1)} %all-to-all-done.1.parts, f32[8,256]{1,0:T(8,128)S(1)} %reshape.17.mass), custom_call_target="tpu_custom_call" | custom-call | flops 16777216 | bytes 8388608 | tf_op jit(solution)/shard_map/pallas_call | solution.py:386
  81.9 2.5 %collective-permute-start.10 = (f32[8,256]{1,0:T(8,128)S(1)}, f32[8,256]{1,0:T(8,128)S(1)}, u32[]{:S(2)}, u32[]{:S(2)}) collective-permute-start(f32[8,256]{1,0:T(8,128)S(1)} %shard_map.81.p0), channel_id=1, source_target_pairs={{0,2},{1,3},{2,0},{3,1},{4,6},{5,7},{6,4},{7,5},{8,10},{9,11},{10,... | collective-permute-start | bytes 24584 | tf_op jit(solution)/shard_map/ppermute | solution.py:404
  84.3 2.7 %collective-permute-start.9 = (f32[8,256]{1,0:T(8,128)S(1)}, f32[8,256]{1,0:T(8,128)S(1)}, u32[]{:S(2)}, u32[]{:S(2)}) collective-permute-start(f32[8,256]{1,0:T(8,128)S(1)} %shard_map.81.p0), channel_id=1, source_target_pairs={{0,3},{1,0},{2,1},{3,2},{4,7},{5,4},{6,5},{7,6},{8,11},{9,8},{10,9... | collective-permute-start | bytes 24584 | tf_op jit(solution)/shard_map/ppermute | solution.py:404
  87.1 1.0 collective-permute-done.8.p1
  88.0 4.8 %shard_map.82 = (f32[8,256]{1,0:T(8,128)S(1)}, f32[8,256]{1,0:T(8,128)S(1)}, f32[4,8,32,512]{3,2,1,0:T(8,128)S(1)}, f32[4,8,32,512]{3,2,1,0:T(8,128)}) custom-call(s32[1]{0:T(128)S(6)} %copy.8.cnt, s32[16]{0:T(128)S(1)} %add_bitcast_fusion.pairs, s32[4]{0:T(128)S(1)} %pad_add_fusion.place, f32[16,256,256]{2,1,0:T(8,128)} %get-tuple-element.32.held, ...), custom_call_target="tpu_custom_call" | custom-call | flops 2147483648 | bytes 8388608 | tf_op jit(solution)/shard_map/pallas_call | solution.py:386
  92.8 10.3 %collective-permute-start.18 = (f32[4,8,32,512]{3,2,1,0:T(8,128)}, f32[4,8,32,512]{3,2,1,0:T(8,128)}, u32[]{:S(2)}, u32[]{:S(2)}) collective-permute-start(f32[4,8,32,512]{3,2,1,0:T(8,128)} %get-tuple-element.45), channel_id=1, source_target_pairs={{0,4},{4,0},{1,5},{5,1},{2,6},{6,2},{3,7},{7,3},{8,12},{12,8},{9,1... | collective-permute-start | bytes 6291464 | tf_op jit(solution)/shard_map/ppermute | solution.py:404
  103.2 4.0 %collective-permute-done.11 = f32[8,256]{1,0:T(8,128)S(1)} collective-permute-done((f32[8,256]{1,0:T(8,128)S(1)}, f32[8,256]{1,0:T(8,128)S(1)}, u32[]{:S(2)}, u32[]{:S(2)}) %collective-permute-start.11) | collective-permute-done | bytes 8224 | tf_op jit(solution)/shard_map/ppermute | solution.py:404
  108.0 3.9 %all-to-all-start.2 = ((f32[32,8,256]{2,1,0:T(8,128)}), f32[32,8,256]{2,1,0:T(8,128)S(1)}, u32[]{:S(2)}, u32[]{:S(2)}) async-start(f32[32,8,256]{2,1,0:T(8,128)} %broadcast_in_dim.8), calls=%async_computation.2 | async-start | bytes 524288 | tf_op jit(solution)/shard_map/all_to_all | solution.py:415
  111.8 2.5 %shard_map.86 = (f32[4,32,512]{2,1,0:T(8,128)S(1)}, f32[4,32,512]{2,1,0:T(8,128)S(1)}, f32[4,32,512]{2,1,0:T(8,128)S(1)}, f32[4,32,512]{2,1,0:T(8,128)}, f32[4,3...) custom-call(f32[4,8,32,512]{3,2,1,0:T(8,128)S(1)} %get-tuple-element.44.keep,, ...), custom_call_target="tpu_custom_call" | custom-call | flops 16777216 | bytes 8388608 | tf_op jit(solution)/shard_map/pallas_call | solution.py:386
  114.4 1.2 collective-permute-start.19
  115.5 1.5 collective-permute-start.23
  117.0 1.3 collective-permute-start.21
  118.3 6.9 %collective-permute-done.19 = f32[4,32,512]{2,1,0:T(8,128)S(1)} collective-permute-done((f32[4,32,512]{2,1,0:T(8,128)S(1)}, f32[4,32,512]{2,1,0:T(8,128)S(1)}, u32[]{:S(2)}, u32[]{:S(2)}) %collective-permute-start.19) | collective-permute-done | bytes 262176 | tf_op jit(solution)/shard_map/ppermute | solution.py:404
  125.4 1.3 collective-permute-start.22
  126.7 1.5 collective-permute-start.24
  128.2 4.1 %shard_map.84 = (f32[264,512]{1,0:T(8,128)S(1)}, f32[264,512]{1,0:T(8,128)S(1)}, f32[264,512]{1,0:T(8,128)}, f32[264,512]{1,0:T(8,128)S(1)}) custom-call(s32[1]{0:T(128)S(6)} %copy.8.cnt, s32[16]{0:T(128)S(1)} %add_bitcast_fusion.pairs, s32[4]{0:T(128)S(1)} %pad_add_fusion.place, f32[16,256,256]{2,1,0:T(8,128)} %get-tuple-element.32.held, ...), custom_call_target="tpu_custom_call" | custom-call | flops 536870912 | bytes 8388608 | tf_op jit(solution)/shard_map/pallas_call | solution.py:386
  132.3 3.9 %collective-permute-start.16 = (f32[264,512]{1,0:T(8,128)}, f32[264,512]{1,0:T(8,128)}, u32[]{:S(2)}, u32[]{:S(2)}) collective-permute-start(f32[264,512]{1,0:T(8,128)} %get-tuple-element.43), channel_id=1, source_target_pairs={{0,3},{1,0},{2,1},{3,2},{4,7},{5,4},{6,5},{7,6},{8,11},{9,8},{10,9... | collective-permute-start | bytes 1622024 | tf_op jit(solution)/shard_map/ppermute | solution.py:404
  136.2 1.0 add_add_fusion.1
  137.2 1.8 %collective-permute-done.22 = f32[4,32,512]{2,1,0:T(8,128)} collective-permute-done((f32[4,32,512]{2,1,0:T(8,128)}, f32[4,32,512]{2,1,0:T(8,128)}, u32[]{:S(2)}, u32[]{:S(2)}) %collective-permute-start.22) | collective-permute-done | bytes 262176 | tf_op jit(solution)/shard_map/ppermute | solution.py:404
  139.0 1.1 add_add_fusion
  140.9 5.7 %all-to-all-start.3 = ((f32[8,32,512]{2,1,0:T(8,128)}), f32[8,32,512]{2,1,0:T(8,128)S(1)}, u32[]{:S(2)}, u32[]{:S(2)}) async-start(f32[8,32,512]{2,1,0:T(8,128)} %pad_maximum_fusion), calls=%async_computation.3 | async-start | bytes 1048576 | tf_op jit(solution)/shard_map/all_to_all | solution.py:532
  146.6 2.3 %collective-permute-start.14 = (f32[264,512]{1,0:T(8,128)S(1)}, f32[264,512]{1,0:T(8,128)S(1)}, u32[]{:S(2)}, u32[]{:S(2)}) collective-permute-start(f32[264,512]{1,0:T(8,128)S(1)} %get-tuple-element.39), channel_id=1, source_target_pairs={{0,3},{1,0},{2,1},{3,2},{4,7},{5,4},{6,5},{7,6},{8,11},{9,8},{10,9... | collective-permute-start | bytes 1622024 | tf_op jit(solution)/shard_map/ppermute | solution.py:404
  148.9 3.5 %shard_map.83 = (f32[264,512]{1,0:T(8,128)S(1)}, f32[264,512]{1,0:T(8,128)S(1)}, f32[264,512]{1,0:T(8,128)S(1)}, f32[264,512]{1,0:T(8,128)S(1)}) custom-call(s32[1]{0:T(128)S(6)} %copy.8.cnt, s32[16]{0:T(128)S(1)} %add_bitcast_fusion.pairs, s32[4]{0:T(128)S(1)} %pad_add_fusion.place, f32[16,256,256]{2,1,0:T(8,128)} %get-tuple-element.32.held, ...), custom_call_target="tpu_custom_call" | custom-call | flops 536870912 | bytes 8388608 | tf_op jit(solution)/shard_map/pallas_call | solution.py:386
  152.4 1.1 add.48
  153.6 4.1 %collective-permute-start.17 = (f32[264,512]{1,0:T(8,128)S(1)}, f32[264,512]{1,0:T(8,128)S(1)}, u32[]{:S(2)}, u32[]{:S(2)}) collective-permute-start(f32[264,512]{1,0:T(8,128)S(1)} %add.48), channel_id=1, source_target_pairs={{0,3},{1,0},{2,1},{3,2},{4,7},{5,4},{6,5},{7,6},{8,11},{9,8},{10,9... | collective-permute-start | bytes 1622024 | tf_op jit(solution)/shard_map/ppermute | solution.py:404
  157.7 1.1 add.47
  158.9 1.8 %collective-permute-done.15.refs_4_ = f32[264,512]{1,0:T(8,128)S(1)} collective-permute-done((f32[264,512]{1,0:T(8,128)S(1)}, f32[264,512]{1,0:T(8,128)S(1)}, u32[]{:S(2)}, u32[]{:S(2)}) %collective-permute-start.15) | collective-permute-done | bytes 540704 | tf_op jit(solution)/shard_map/ppermute | solution.py:404
  160.7 9.1 %collective-permute-done.17.refs_5_ = f32[264,512]{1,0:T(8,128)S(1)} collective-permute-done((f32[264,512]{1,0:T(8,128)S(1)}, f32[264,512]{1,0:T(8,128)S(1)}, u32[]{:S(2)}, u32[]{:S(2)}) %collective-permute-start.17) | collective-permute-done | bytes 540704 | tf_op jit(solution)/shard_map/ppermute | solution.py:404
  169.7 3.6 %collective-permute-done.13.refs_1_ = f32[264,512]{1,0:T(8,128)S(1)} collective-permute-done((f32[264,512]{1,0:T(8,128)S(1)}, f32[264,512]{1,0:T(8,128)S(1)}, u32[]{:S(2)}, u32[]{:S(2)}) %collective-permute-start.13) | collective-permute-done | bytes 540704 | tf_op jit(solution)/shard_map/ppermute | solution.py:404
  173.3 1.3 shard_map.85
  174.7 1.4 shard_map.87
  (42 shorter events, 6.1 us)
Async XLA Ops:
  2.0 11.4 %copy-start = (f32[2048]{0:T(1024)S(1)}, f32[2048]{0:T(1024)}, u32[]{:S(2)}) copy-start(f32[2048]{0:T(1024)} %param.8) | copy-start | bytes 24580
  6.2 7.2 %collective-permute-start = (f32[8,256]{1,0:T(8,128)S(1)}, f32[8,256]{1,0:T(8,128)S(1)}, u32[]{:S(2)}, u32[]{:S(2)}) collective-permute-start(f32[8,256]{1,0:T(8,128)S(1)} %get-tuple-element.29.p0), channel_id=1, source_target_pairs={{0,1},{1,2},{2,3},{3,0},{4,5},{5,6},{6,7},{7,4},{8,9},{9,10},{10,1... | collective-permute-start | bytes 24584 | tf_op jit(solution)/shard_map/ppermute | solution.py:404
  8.3 5.1 %collective-permute-start.1 = (f32[8,256]{1,0:T(8,128)S(1)}, f32[8,256]{1,0:T(8,128)S(1)}, u32[]{:S(2)}, u32[]{:S(2)}) collective-permute-start(f32[8,256]{1,0:T(8,128)S(1)} %get-tuple-element.29.p0), channel_id=1, source_target_pairs={{0,3},{1,0},{2,1},{3,2},{4,7},{5,4},{6,5},{7,6},{8,11},{9,8},{10,9... | collective-permute-start | bytes 24584 | tf_op jit(solution)/shard_map/ppermute | solution.py:404
  11.8 4.0 %collective-permute-start.2 = (f32[8,256]{1,0:T(8,128)S(1)}, f32[8,256]{1,0:T(8,128)S(1)}, u32[]{:S(2)}, u32[]{:S(2)}) collective-permute-start(f32[8,256]{1,0:T(8,128)S(1)} %get-tuple-element.29.p0), channel_id=1, source_target_pairs={{0,2},{1,3},{2,0},{3,1},{4,6},{5,7},{6,4},{7,5},{8,10},{9,11},{10,... | collective-permute-start | bytes 24584 | tf_op jit(solution)/shard_map/ppermute | solution.py:404
  15.8 19.3 %copy-start.1 = (f32[2048]{0:T(1024)S(1)}, f32[2048]{0:T(1024)}, u32[]{:S(2)}) copy-start(f32[2048]{0:T(1024)} %param.9) | copy-start | bytes 24580
  17.7 8.8 %collective-permute-start.3 = (f32[8,256]{1,0:T(8,128)S(1)}, f32[8,256]{1,0:T(8,128)S(1)}, u32[]{:S(2)}, u32[]{:S(2)}) collective-permute-start(f32[8,256]{1,0:T(8,128)S(1)} %get-tuple-element.30), channel_id=1, source_target_pairs={{0,4},{4,0},{1,5},{5,1},{2,6},{6,2},{3,7},{7,3},{8,12},{12,8},{9,1... | collective-permute-start | bytes 24584 | tf_op jit(solution)/shard_map/ppermute | solution.py:404
  27.3 17.9 %all-to-all-start = ((f32[32,8,256]{2,1,0:T(8,128)}), f32[32,8,256]{2,1,0:T(8,128)S(1)}, u32[]{:S(2)}, u32[]{:S(2)}) async-start(f32[32,8,256]{2,1,0:T(8,128)} %broadcast_in_dim.6), calls=%async_computation | async-start | bytes 524288 | tf_op jit(solution)/shard_map/all_to_all | solution.py:415
  47.8 5.0 %collective-permute-start.4 = (f32[8,256]{1,0:T(8,128)S(1)}, f32[8,256]{1,0:T(8,128)S(1)}, u32[]{:S(2)}, u32[]{:S(2)}) collective-permute-start(f32[8,256]{1,0:T(8,128)S(1)} %get-tuple-element.33.p0), channel_id=1, source_target_pairs={{0,1},{1,2},{2,3},{3,0},{4,5},{5,6},{6,7},{7,4},{8,9},{9,10},{10,1... | collective-permute-start | bytes 24584 | tf_op jit(solution)/shard_map/ppermute | solution.py:404
  47.9 4.9 %collective-permute-start.5 = (f32[8,256]{1,0:T(8,128)S(1)}, f32[8,256]{1,0:T(8,128)S(1)}, u32[]{:S(2)}, u32[]{:S(2)}) collective-permute-start(f32[8,256]{1,0:T(8,128)S(1)} %get-tuple-element.33.p0), channel_id=1, source_target_pairs={{0,3},{1,0},{2,1},{3,2},{4,7},{5,4},{6,5},{7,6},{8,11},{9,8},{10,9... | collective-permute-start | bytes 24584 | tf_op jit(solution)/shard_map/ppermute | solution.py:404
  50.6 4.0 %collective-permute-start.6 = (f32[8,256]{1,0:T(8,128)S(1)}, f32[8,256]{1,0:T(8,128)S(1)}, u32[]{:S(2)}, u32[]{:S(2)}) collective-permute-start(f32[8,256]{1,0:T(8,128)S(1)} %get-tuple-element.33.p0), channel_id=1, source_target_pairs={{0,2},{1,3},{2,0},{3,1},{4,6},{5,7},{6,4},{7,5},{8,10},{9,11},{10,... | collective-permute-start | bytes 24584 | tf_op jit(solution)/shard_map/ppermute | solution.py:404
  56.3 8.5 %collective-permute-start.7 = (f32[8,256]{1,0:T(8,128)S(1)}, f32[8,256]{1,0:T(8,128)S(1)}, u32[]{:S(2)}, u32[]{:S(2)}) collective-permute-start(f32[8,256]{1,0:T(8,128)S(1)} %shard_map.80), channel_id=1, source_target_pairs={{0,4},{4,0},{1,5},{5,1},{2,6},{6,2},{3,7},{7,3},{8,12},{12,8},{9,1... | collective-permute-start | bytes 24584 | tf_op jit(solution)/shard_map/ppermute | solution.py:404
  65.6 14.1 %all-to-all-start.1 = ((f32[32,8,256]{2,1,0:T(8,128)}), f32[32,8,256]{2,1,0:T(8,128)S(1)}, u32[]{:S(2)}, u32[]{:S(2)}) async-start(f32[32,8,256]{2,1,0:T(8,128)} %broadcast_in_dim.7), calls=%async_computation.1 | async-start | bytes 524288 | tf_op jit(solution)/shard_map/all_to_all | solution.py:415
  81.9 5.2 %collective-permute-start.10 = (f32[8,256]{1,0:T(8,128)S(1)}, f32[8,256]{1,0:T(8,128)S(1)}, u32[]{:S(2)}, u32[]{:S(2)}) collective-permute-start(f32[8,256]{1,0:T(8,128)S(1)} %shard_map.81.p0), channel_id=1, source_target_pairs={{0,2},{1,3},{2,0},{3,1},{4,6},{5,7},{6,4},{7,5},{8,10},{9,11},{10,... | collective-permute-start | bytes 24584 | tf_op jit(solution)/shard_map/ppermute | solution.py:404
  84.3 3.7 %collective-permute-start.8 = (f32[8,256]{1,0:T(8,128)S(1)}, f32[8,256]{1,0:T(8,128)S(1)}, u32[]{:S(2)}, u32[]{:S(2)}) collective-permute-start(f32[8,256]{1,0:T(8,128)S(1)} %shard_map.81.p0), channel_id=1, source_target_pairs={{0,1},{1,2},{2,3},{3,0},{4,5},{5,6},{6,7},{7,4},{8,9},{9,10},{10,1... | collective-permute-start | bytes 24584 | tf_op jit(solution)/shard_map/ppermute | solution.py:404
  84.3 3.7 %collective-permute-start.9 = (f32[8,256]{1,0:T(8,128)S(1)}, f32[8,256]{1,0:T(8,128)S(1)}, u32[]{:S(2)}, u32[]{:S(2)}) collective-permute-start(f32[8,256]{1,0:T(8,128)S(1)} %shard_map.81.p0), channel_id=1, source_target_pairs={{0,3},{1,0},{2,1},{3,2},{4,7},{5,4},{6,5},{7,6},{8,11},{9,8},{10,9... | collective-permute-start | bytes 24584 | tf_op jit(solution)/shard_map/ppermute | solution.py:404
  92.8 19.0 %collective-permute-start.18 = (f32[4,8,32,512]{3,2,1,0:T(8,128)}, f32[4,8,32,512]{3,2,1,0:T(8,128)}, u32[]{:S(2)}, u32[]{:S(2)}) collective-permute-start(f32[4,8,32,512]{3,2,1,0:T(8,128)} %get-tuple-element.45), channel_id=1, source_target_pairs={{0,4},{4,0},{1,5},{5,1},{2,6},{6,2},{3,7},{7,3},{8,12},{12,8},{9,1... | collective-permute-start | bytes 6291464 | tf_op jit(solution)/shard_map/ppermute | solution.py:404
  103.1 4.1 %collective-permute-start.11 = (f32[8,256]{1,0:T(8,128)S(1)}, f32[8,256]{1,0:T(8,128)S(1)}, u32[]{:S(2)}, u32[]{:S(2)}) collective-permute-start(f32[8,256]{1,0:T(8,128)S(1)} %get-tuple-element.34), channel_id=1, source_target_pairs={{0,4},{4,0},{1,5},{5,1},{2,6},{6,2},{3,7},{7,3},{8,12},{12,8},{9,1... | collective-permute-start | bytes 24584 | tf_op jit(solution)/shard_map/ppermute | solution.py:404
  108.0 20.2 %all-to-all-start.2 = ((f32[32,8,256]{2,1,0:T(8,128)}), f32[32,8,256]{2,1,0:T(8,128)S(1)}, u32[]{:S(2)}, u32[]{:S(2)}) async-start(f32[32,8,256]{2,1,0:T(8,128)} %broadcast_in_dim.8), calls=%async_computation.2 | async-start | bytes 524288 | tf_op jit(solution)/shard_map/all_to_all | solution.py:415
  114.4 10.8 %collective-permute-start.19 = (f32[4,32,512]{2,1,0:T(8,128)S(1)}, f32[4,32,512]{2,1,0:T(8,128)S(1)}, u32[]{:S(2)}, u32[]{:S(2)}) collective-permute-start(f32[4,32,512]{2,1,0:T(8,128)S(1)} %get-tuple-element.48), channel_id=1, source_target_pairs={{0,64},{64,128},{128,192},{192,0},{1,65},{65,129},{129,193},{193,1... | collective-permute-start | bytes 786440 | tf_op jit(solution)/shard_map/ppermute | solution.py:404
  115.5 11.1 %collective-permute-start.23 = (f32[4,32,512]{2,1,0:T(8,128)S(1)}, f32[4,32,512]{2,1,0:T(8,128)S(1)}, u32[]{:S(2)}, u32[]{:S(2)}) collective-permute-start(f32[4,32,512]{2,1,0:T(8,128)S(1)} %get-tuple-element.53), channel_id=1, source_target_pairs={{0,192},{64,0},{128,64},{192,128},{1,193},{65,1},{129,65},{193,129... | collective-permute-start | bytes 786440 | tf_op jit(solution)/shard_map/ppermute | solution.py:404
  117.0 19.1 %collective-permute-start.21 = (f32[4,32,512]{2,1,0:T(8,128)}, f32[4,32,512]{2,1,0:T(8,128)S(1)}, u32[]{:S(2)}, u32[]{:S(2)}) collective-permute-start(f32[4,32,512]{2,1,0:T(8,128)} %get-tuple-element.49), channel_id=1, source_target_pairs={{0,192},{64,0},{128,64},{192,128},{1,193},{65,1},{129,65},{193,129... | collective-permute-start | bytes 786440 | tf_op jit(solution)/shard_map/ppermute | solution.py:404
  125.2 11.0 %collective-permute-start.20 = (f32[4,32,512]{2,1,0:T(8,128)S(1)}, f32[4,32,512]{2,1,0:T(8,128)}, u32[]{:S(2)}, u32[]{:S(2)}) collective-permute-start(f32[4,32,512]{2,1,0:T(8,128)S(1)} %add.49), channel_id=1, source_target_pairs={{0,64},{64,128},{128,192},{192,0},{1,65},{65,129},{129,193},{193,1... | collective-permute-start | bytes 786440 | tf_op jit(solution)/shard_map/ppermute | solution.py:404
  125.4 13.6 %collective-permute-start.22 = (f32[4,32,512]{2,1,0:T(8,128)}, f32[4,32,512]{2,1,0:T(8,128)}, u32[]{:S(2)}, u32[]{:S(2)}) collective-permute-start(f32[4,32,512]{2,1,0:T(8,128)} %get-tuple-element.51), channel_id=1, source_target_pairs={{0,64},{64,128},{128,192},{192,0},{1,65},{65,129},{129,193},{193,1... | collective-permute-start | bytes 786440 | tf_op jit(solution)/shard_map/ppermute | solution.py:404
  126.7 12.2 %collective-permute-start.24 = (f32[4,32,512]{2,1,0:T(8,128)S(1)}, f32[4,32,512]{2,1,0:T(8,128)}, u32[]{:S(2)}, u32[]{:S(2)}) collective-permute-start(f32[4,32,512]{2,1,0:T(8,128)S(1)} %add.53), channel_id=1, source_target_pairs={{0,192},{64,0},{128,64},{192,128},{1,193},{65,1},{129,65},{193,129... | collective-permute-start | bytes 786440 | tf_op jit(solution)/shard_map/ppermute | solution.py:404
  132.3 20.2 %collective-permute-start.16 = (f32[264,512]{1,0:T(8,128)}, f32[264,512]{1,0:T(8,128)}, u32[]{:S(2)}, u32[]{:S(2)}) collective-permute-start(f32[264,512]{1,0:T(8,128)} %get-tuple-element.43), channel_id=1, source_target_pairs={{0,3},{1,0},{2,1},{3,2},{4,7},{5,4},{6,5},{7,6},{8,11},{9,8},{10,9... | collective-permute-start | bytes 1622024 | tf_op jit(solution)/shard_map/ppermute | solution.py:404
  136.2 21.5 %collective-permute-start.12 = (f32[264,512]{1,0:T(8,128)S(1)}, f32[264,512]{1,0:T(8,128)}, u32[]{:S(2)}, u32[]{:S(2)}) collective-permute-start(f32[264,512]{1,0:T(8,128)S(1)} %get-tuple-element.38), channel_id=1, source_target_pairs={{0,1},{1,2},{2,3},{3,0},{4,5},{5,6},{6,7},{7,4},{8,9},{9,10},{10,1... | collective-permute-start | bytes 1622024 | tf_op jit(solution)/shard_map/ppermute | solution.py:404
  140.9 33.8 %all-to-all-start.3 = ((f32[8,32,512]{2,1,0:T(8,128)}), f32[8,32,512]{2,1,0:T(8,128)S(1)}, u32[]{:S(2)}, u32[]{:S(2)}) async-start(f32[8,32,512]{2,1,0:T(8,128)} %pad_maximum_fusion), calls=%async_computation.3 | async-start | bytes 1048576 | tf_op jit(solution)/shard_map/all_to_all | solution.py:532
  146.6 12.3 %collective-permute-start.14 = (f32[264,512]{1,0:T(8,128)S(1)}, f32[264,512]{1,0:T(8,128)S(1)}, u32[]{:S(2)}, u32[]{:S(2)}) collective-permute-start(f32[264,512]{1,0:T(8,128)S(1)} %get-tuple-element.39), channel_id=1, source_target_pairs={{0,3},{1,0},{2,1},{3,2},{4,7},{5,4},{6,5},{7,6},{8,11},{9,8},{10,9... | collective-permute-start | bytes 1622024 | tf_op jit(solution)/shard_map/ppermute | solution.py:404
  148.9 11.8 %collective-permute-start.15 = (f32[264,512]{1,0:T(8,128)S(1)}, f32[264,512]{1,0:T(8,128)S(1)}, u32[]{:S(2)}, u32[]{:S(2)}) collective-permute-start(f32[264,512]{1,0:T(8,128)S(1)} %get-tuple-element.41), channel_id=1, source_target_pairs={{0,1},{1,2},{2,3},{3,0},{4,5},{5,6},{6,7},{7,4},{8,9},{9,10},{10,1... | collective-permute-start | bytes 1622024 | tf_op jit(solution)/shard_map/ppermute | solution.py:404
  153.6 16.2 %collective-permute-start.17 = (f32[264,512]{1,0:T(8,128)S(1)}, f32[264,512]{1,0:T(8,128)S(1)}, u32[]{:S(2)}, u32[]{:S(2)}) collective-permute-start(f32[264,512]{1,0:T(8,128)S(1)} %add.48), channel_id=1, source_target_pairs={{0,3},{1,0},{2,1},{3,2},{4,7},{5,4},{6,5},{7,6},{8,11},{9,8},{10,9... | collective-permute-start | bytes 1622024 | tf_op jit(solution)/shard_map/ppermute | solution.py:404
  158.8 14.5 %collective-permute-start.13 = (f32[264,512]{1,0:T(8,128)S(1)}, f32[264,512]{1,0:T(8,128)S(1)}, u32[]{:S(2)}, u32[]{:S(2)}) collective-permute-start(f32[264,512]{1,0:T(8,128)S(1)} %add.47), channel_id=1, source_target_pairs={{0,1},{1,2},{2,3},{3,0},{4,5},{5,6},{6,7},{7,4},{8,9},{9,10},{10,1... | collective-permute-start | bytes 1622024 | tf_op jit(solution)/shard_map/ppermute | solution.py:404

commit v2 on v1

--- a/solution.py
+++ b/solution.py
@@ -35,6 +35,23 @@
     peak = jnp.max(ref[...], axis=0)
     total = jnp.sum(jnp.exp(ref[...] - peak[None]), axis=0)
     return peak + jnp.log(total)
+
+
+def sum_stack(ref):
+    return jnp.sum(ref[...], axis=0)
+
+
+def both_halves(place, mine, other, join):
+    first = place[2] == 0
+    a, b = join(mine), join(other)
+    return jnp.concatenate([jnp.where(first, a, b), jnp.where(first, b, a)], axis=1)
+
+
+def hand_out(place, stats, mine, give):
+    first = place[2] == 0
+    low, high = stats[:, :128], stats[:, 128:]
+    mine[...] = jnp.where(first, low, high)
+    give[...] = jnp.where(first, high, low)
 
 
 def slots(cnt, pairs, body):
@@ -159,10 +176,11 @@
 
 
 def plan_kernel(
-    cnt, pairs, held, parts, mass, u, plan, out, v_ref, u_ref, s_ref, scores, sem, out_sem
+    cnt, pairs, place, held, mine, other, mass, u, plan, out,
+    v_ref, u_ref, s_ref, scores, sem, out_sem,
 ):
     arrive = fetch_scores(cnt, held, scores, sem)
-    v_ref[...] = mass[...] - lse_stack(parts)
+    v_ref[...] = mass[...] - both_halves(place, mine, other, lse_stack)
     spread_columns(u[...], u_ref)
 
     def tile_of(k, a, b, rows):
@@ -180,9 +198,9 @@
     every_slot(cnt, lambda k: pltpu.make_async_copy(scores.at[k], plan.at[k], out_sem.at[k]).wait())
 
 
-def row_kernel(cnt, pairs, held, parts, mass, out, b_ref, s_ref, plan, sem):
+def row_kernel(cnt, pairs, place, held, mine, other, mass, out, b_ref, s_ref, plan, sem):
     arrive = fetch_scores(cnt, held, plan, sem)
-    b_ref[...] = jnp.exp(mass[...]) / jnp.sum(parts[...], axis=0)
+    b_ref[...] = jnp.exp(mass[...]) / both_halves(place, mine, other, sum_stack)
 
     def tile_of(k, a, b, rows):
         if rows.start == 0:
@@ -212,14 +230,17 @@
         m_ref[b] = jnp.broadcast_to(jnp.max(m_ref[b], axis=0, keepdims=True), (8, BLK))
 
 
-def col_lse(m_ref, s_ref, lse_out):
+def col_lse(place, m_ref, s_ref, mine, give):
+    rows = []
     for b in range(NB):
         total = jnp.sum(s_ref[b], axis=0, keepdims=True)
-        lse_out[b : b + 1, :] = jnp.where(total > 0, m_ref[b, :1, :] + jnp.log(total), FLOOR)
+        rows.append(jnp.where(total > 0, m_ref[b, :1, :] + jnp.log(total), FLOOR))
+    hand_out(place, jnp.concatenate(rows, axis=0), mine, give)
 
 
 def col_kernel(
-    cnt, pairs, held, p0, p1, p2, p3, mass, lse_out, u_out, u_ref, m_ref, s_ref, scores, sem
+    cnt, pairs, place, held, p0, p1, p2, p3, mass, mine, give, u_out,
+    u_ref, m_ref, s_ref, scores, sem,
 ):
     arrive = fetch_scores(cnt, held, scores, sem)
     u = mass[...] - lse_of([p0[...], p1[...], p2[...], p3[...]])
@@ -238,10 +259,17 @@
             s_ref[b, :, lanes] = total
 
     slots(cnt, pairs, totals)
-    col_lse(m_ref, s_ref, lse_out)
-
-
-def col_sum_kernel(cnt, pairs, held, p0, p1, p2, p3, mass, out, a_ref, s_ref, plan, sem):
+    col_lse(place, m_ref, s_ref, mine, give)
+
+
+def hand_out_sums(place, s_ref, mine, give):
+    sums = [jnp.sum(s_ref[b], axis=0, keepdims=True) for b in range(NB)]
+    hand_out(place, jnp.concatenate(sums, axis=0), mine, give)
+
+
+def col_sum_kernel(
+    cnt, pairs, place, held, p0, p1, p2, p3, mass, mine, give, a_ref, s_ref, plan, sem
+):
     arrive = fetch_scores(cnt, held, plan, sem)
     spread_columns(jnp.exp(mass[...]) / (p0[...] + p1[...] + p2[...] + p3[...]), a_ref)
     s_ref[...] = jnp.zeros(s_ref.shape, f32)
@@ -257,12 +285,11 @@
             s_ref[b, :, lanes] = total
 
     slots(cnt, pairs, body)
-    for b in range(NB):
-        out[b : b + 1, :] = jnp.sum(s_ref[b], axis=0, keepdims=True)
+    hand_out_sums(place, s_ref, mine, give)
 
 
 def last_col_kernel(
-    cnt, pairs, place, held, p0, p1, p2, p3, mass, text, out, a_out, keep, send,
+    cnt, pairs, place, held, p0, p1, p2, p3, mass, text, mine, give, a_out, keep, send,
     a_ref, s_ref, plan, sem, texts, tsem, w_ref, acc,
 ):
     arrive = fetch_scores(cnt, held, plan, sem)
@@ -290,8 +317,7 @@
         )
 
     slots(cnt, pairs, body)
-    for b in range(NB):
-        out[b : b + 1, :] = jnp.sum(s_ref[b], axis=0, keepdims=True)
+    hand_out_sums(place, s_ref, mine, give)
     y, c = place[1], place[2]
     for r in range(NY):
         b0 = 2 * lax.rem(y + r, NY)
@@ -307,60 +333,76 @@
             outs[2 * r + h][...] = keep[r, 4 * h : 4 * h + 4] + got[r, 4 * h : 4 * h + 4]
 
 
-def tgt_norm_kernel(place, parts, stack, out, c_ref):
+def tgt_norm_kernel(place, parts, mine, other, out, c_ref):
     y, c, z = place[1], place[2], place[3]
     b = 2 * y + z // 4
     lane = lax.broadcasted_iota(jnp.int32, (BLK, 128), 1)
-    cols = to_columns(jnp.sum(stack[...], axis=0))
+    cols = to_columns(both_halves(place, mine, other, sum_stack))
     c_ref[...] = jnp.where(lane == b, cols, 0.0)
     rows = pl.ds(pl.multiple_of(lax.rem(z, 4) * 64 + c * 32, 32), 32)
     mass = jnp.sum(c_ref[rows, :], axis=1, keepdims=True)
     out[...] = jnp.sum(parts[...], axis=0) / mass
 
 
-def final_kernel(offset, cnt, pairs, place, held, parts, mass, scale, image, *refs):
-    src_out = refs[:4]
-    scores, sem, images, isem, b_ref, a_ref, w_ref, acc, rsum = refs[4:]
+def final_kernel(
+    offset, n, cnt, pairs, place, held, mine, other, mass, scale, image, *refs
+):
+    src_out = refs[:n]
+    plan, sem, images, isem, b_ref, r_ref, a_ref, w_ref, acc, rsum = refs[n:]
     start = 2 * place[0] + offset
 
-    def mine(act):
+    def chosen(act):
         def step(k, _):
             pair = pairs[k]
-            a = pair // NB
-            q = lax.rem(a + 2 * NB - start, NB)
-
-            @pl.when(q < 4)
+            q = lax.rem(pair // NB + 2 * NB - start, NB)
+
+            @pl.when(q < n)
             def _():
-                act(k, q, a, pair % NB)
+                act(k, q, pair % NB)
 
             return 0
 
         lax.fori_loop(0, cnt[0], step, 0)
 
-    mine(lambda k, q, a, b: pltpu.make_async_copy(held.at[k], scores.at[k], sem.at[k]).start())
-    copies = fetch_blocks(image, images, isem)
-    b_ref[...] = jnp.exp(mass[...]) / jnp.sum(parts[...], axis=0)
-    spread_columns(scale[...], a_ref)
+    def copies(k, b):
+        return (
+            pltpu.make_async_copy(held.at[k], plan.at[k], sem.at[k]),
+            pltpu.make_async_copy(
+                image.at[pl.ds(pl.multiple_of(b * BLK, BLK), BLK), :], images.at[k], isem.at[k]
+            ),
+        )
+
+    @chosen
+    def _(k, q, b):
+        for copy in copies(k, b):
+            copy.start()
+
+    b_ref[...] = jnp.exp(mass[...]) / both_halves(place, mine, other, sum_stack)
+    r_ref[...] = jnp.zeros(r_ref.shape, f32)
+    for q in range(n):
+        r_ref[q : q + 1, :] = scale[pl.ds(lax.rem(start + q, NB), 1), :]
+    cols = to_columns(r_ref[...])
+    for q in range(n):
+        a_ref[q] = jnp.broadcast_to(cols[:, q : q + 1], (BLK, 128))
     acc[...] = jnp.zeros(acc.shape, f32)
     rsum[...] = jnp.zeros(rsum.shape, f32)
-    for copy in copies:
-        copy.wait()
-
-    def body(k, q, a, b):
-        pltpu.make_async_copy(held.at[k], scores.at[k], sem.at[k]).wait()
+
+    @chosen
+    def _(k, q, b):
+        for copy in copies(k, b):
+            copy.wait()
         v = b_ref[pl.ds(b, 1), :]
         for r in range(0, BLK, STEP):
             rows = slice(r, r + STEP)
             for half in range(2):
                 lanes = slice(half * 128, half * 128 + 128)
-                plan = scores[k, rows, lanes] * a_ref[a, rows, :] * v[:, lanes]
-                rsum[q, rows, :] += plan
-                w_ref[rows, lanes] = plan.astype(jnp.bfloat16)
-        acc[q] += jnp.dot(w_ref[...], images[b], preferred_element_type=f32)
-
-    mine(body)
-    masses = columns_to_rows([jnp.sum(rsum[q], axis=1, keepdims=True) for q in range(4)])
-    for q in range(4):
+                tile = plan[k, rows, lanes] * a_ref[q, rows, :] * v[:, lanes]
+                rsum[q, rows, :] += tile
+                w_ref[rows, lanes] = tile.astype(jnp.bfloat16)
+        acc[q] += jnp.dot(w_ref[...], images[k], preferred_element_type=f32)
+
+    masses = columns_to_rows([jnp.sum(rsum[q], axis=1, keepdims=True) for q in range(n)])
+    for q in range(n):
         src_out[q][:BLK, :] = acc[q]
         src_out[q][BLK:, :BLK] = jnp.broadcast_to(masses[q : q + 1, :], (8, BLK))
         src_out[q][BLK:, BLK:] = jnp.zeros((8, D - BLK), f32)
@@ -408,11 +450,12 @@
     return [part] + [shift(part, "x", NX, k) for k in (1, 3, 2)]
 
 
-def over_src(part, join):
-    other = shift(part, "c", NC, 1)
-    both = join([part, other])
-    copies = jnp.broadcast_to(both[None], (NY * NZ, NB, BLK))
-    return lax.all_to_all(copies, ("y", "z"), 0, 0, tiled=True)
+def over_src(mine, give, join):
+    got = shift(give, "c", NC, 1)
+    both = join([mine, got])
+    copies = jnp.broadcast_to(both[None], (NY * NZ, NB, 128))
+    stack = lax.all_to_all(copies, ("y", "z"), 0, 0, tiled=True)
+    return stack, shift(stack, "c", NC, 1)
 
 
 def ring_scatter(own_a, own_b, plus_a, plus_b, far_a, far_b, minus_a, minus_b, axis, size):
@@ -449,45 +492,46 @@
         (2, 3, 4),
         1 << 30,
     )
-    part, u = call(
+    lanes = sds(NB, 128)
+    mine, give, u = call(
         col_kernel,
-        (stats, stats),
-        (count, pairs, scores, *over_x(part), mass_src),
-        2,
+        (lanes, lanes, stats),
+        (count, pairs, place, scores, *over_x(part), mass_src),
+        3,
         col_scratch + tiles,
-        hbm=(2,),
+        hbm=(3,),
     )
-    stack = over_src(part, lse_of)
+    stack = over_src(mine, give, lse_of)
     plan, part = call(
         plan_kernel,
         (sds(CAP, BLK, BLK), stats),
-        (count, pairs, scores, stack, mass_tgt, u),
-        2,
+        (count, pairs, place, scores, *stack, mass_tgt, u),
+        3,
         [pltpu.VMEM((NB, BLK), f32)] + row_scratch + tiles + tiles[1:],
-        hbm=(2, 6),
+        hbm=(3, 8),
     )
     for _ in range(ITERS - 2):
-        part = call(
+        mine, give = call(
             col_sum_kernel,
-            stats,
-            (count, pairs, plan, *over_x(part), mass_src),
-            2,
+            (lanes, lanes),
+            (count, pairs, place, plan, *over_x(part), mass_src),
+            3,
             [col_scratch[0], col_scratch[1]] + tiles,
-            hbm=(2,),
+            hbm=(3,),
         )
-        stack = over_src(part, sum)
+        stack = over_src(mine, give, sum)
         part = call(
             row_kernel,
             stats,
-            (count, pairs, plan, stack, mass_tgt),
-            2,
+            (count, pairs, place, plan, *stack, mass_tgt),
+            3,
             [pltpu.VMEM((NB, BLK), f32), row_scratch[0]] + tiles,
-            hbm=(2,),
+            hbm=(3,),
         )
     half = sds(NY, NZ, 32, D)
-    part, scale, keep, send = call(
+    mine, give, scale, keep, send = call(
         last_col_kernel,
-        (stats, stats, half, half),
+        (lanes, lanes, stats, half, half),
         (count, pairs, place, plan, *over_x(part), mass_src, text),
         3,
         [col_scratch[0], col_scratch[1]]
@@ -500,38 +544,39 @@
         1 << 31,
     )
     got = shift(send, "c", NC, 1)
-    stack = over_src(part, sum)
+    stack = over_src(mine, give, sum)
     halves = call(add_kernel, tuple([sds(4, 32, D)] * 8), (keep, got), 0, (), 16)
 
-    def final(offset):
+    def final(offset, n):
         return call(
-            functools.partial(final_kernel, offset),
-            tuple([sds(BLK + 8, D)] * 4),
-            (count, pairs, place, plan, stack, mass_tgt, scale, image),
+            functools.partial(final_kernel, offset, n),
+            tuple([sds(BLK + 8, D)] * n),
+            (count, pairs, place, plan, *stack, mass_tgt, scale, image),
             3,
             tiles
-            + blocks
-            + block_sem
             + [
+                pltpu.VMEM((CAP, BLK, D), jnp.bfloat16),
+                tiles[1],
                 pltpu.VMEM((NB, BLK), f32),
-                pltpu.VMEM((NB, BLK, 128), f32),
+                pltpu.VMEM((NB, BLK), f32),
+                pltpu.VMEM((n, BLK, 128), f32),
                 pltpu.VMEM((BLK, BLK), jnp.bfloat16),
-                pltpu.VMEM((4, BLK, D), f32),
-                pltpu.VMEM((4, BLK, 128), f32),
+                pltpu.VMEM((n, BLK, D), f32),
+                pltpu.VMEM((n, BLK, 128), f32),
             ],
-            50,
-            (3, 7),
+            51,
+            (3, 8),
             1 << 29,
         )
 
-    far = final(3)
-    near = final(7)
-    part_a, part_b = ring_scatter(*near[1:], *far, near[0], "x", NX)
+    far = final(4, 2)
+    near = final(6, 6)
+    part_a, part_b = ring_scatter(*near[2:], *far, *near[:2], "x", NX)
     tgt_a, tgt_b = ring_scatter(*halves, "y", NY)
     summed = jnp.concatenate([sum(tgt_a), sum(tgt_b)], axis=0)
     got = lax.all_to_all(summed, "z", 0, 0, tiled=True)
     tgt_map = call(
-        tgt_norm_kernel, sds(32, D), (place, got, stack), 1, [pltpu.VMEM((BLK, 128), f32)], 16
+        tgt_norm_kernel, sds(32, D), (place, got, *stack), 1, [pltpu.VMEM((BLK, 128), f32)], 16
     )
     src_map = call(src_norm_kernel, sds(2 * BLK, D), (*part_a, *part_b), 0, (), 16)
     return (src_map, tgt_map)

time: 178 us -> 176 us (0.989)
  the two profiles are of different devices: /device:TPU:1 before, /device:TPU:8 now
where the time goes in v2:
time: 176 us
  waiting for transfers between devices  54.1 us (31%)
  Pallas kernels  44.9 us (26%)
  starting transfers between devices  37.3 us (21%)
  blocking collectives  33.1 us (19%)
  other arithmetic  4.18 us (2%)
    ppermute x28, waiting for transfers between devices, shift(): return lax.ppermute(a, axis, [(i, (i + by) % size) for i in range(size)])  48.1 us
    pallas_call x11, Pallas kernels, call(): pl.pallas_call(kernel, out_shape=outs, in_specs=specs, out_specs=out_spec...  44.9 us
    all_to_all x2, blocking collectives, over_src(): stack = lax.all_to_all(copies, ('y', 'z'), 0, 0, tiled=True)  33.1 us
    ppermute x28, starting transfers between devices, shift(): return lax.ppermute(a, axis, [(i, (i + by) % size) for i in range(size)])  24 us
    all_to_all x1, starting transfers between devices, program(): got = lax.all_to_all(summed, 'z', 0, 0, tiled=True)  6.65 us
    all_to_all x1, starting transfers between devices, over_src(): stack = lax.all_to_all(copies, ('y', 'z'), 0, 0, tiled=True)  6.63 us
    all_to_all x1, waiting for transfers between devices, over_src(): stack = lax.all_to_all(copies, ('y', 'z'), 0, 0, tiled=True)  6.07 us
  transfers between devices with their start and end apart: 30, of which 20 were waited for; matrix products, arithmetic and copies ran while one was open for 2% of the time, Pallas kernels for 6%

profile of v2, /device:TPU:8, one launch (start us, length us, event | category | flops | bytes accessed | tf_op | source)
XLA Modules:
  0.0 175.9 jit_solution(3838680918370825163)
XLA Ops:
  0.6 0.8 add_bitcast_fusion.pairs
  2.1 8.0 %shard_map.77 = (f32[16,256,256]{2,1,0:T(8,128)}, f32[8,256]{1,0:T(8,128)S(1)}) custom-call(s32[1]{0:T(128)S(6)} %copy.8.cnt, s32[16]{0:T(128)S(1)} %add_bitcast_fusion.pairs, bf16[2048,512]{1,0:T(8,128)(2,1)} %text.3, bf16[2048,512]{1,0:T(8,128)(2,1)} %image.5), custom_call_target="tpu_custom_call" | custom-call | flops 1073741824 | bytes 8388608 | tf_op jit(solution)/shard_map/pallas_call | solution.py:428
  10.1 3.2 %collective-permute-start.1 = (f32[8,256]{1,0:T(8,128)S(1)}, f32[8,256]{1,0:T(8,128)S(1)}, u32[]{:S(2)}, u32[]{:S(2)}) collective-permute-start(f32[8,256]{1,0:T(8,128)S(1)} %get-tuple-element.33.p0), channel_id=1, source_target_pairs={{0,3},{1,0},{2,1},{3,2},{4,7},{5,4},{6,5},{7,6},{8,11},{9,8},{10,9... | collective-permute-start | bytes 24584 | tf_op jit(solution)/shard_map/ppermute | solution.py:446
  13.3 1.0 collective-permute-start.2
  14.4 0.6 collective-permute-done.p1
  15.0 3.5 %collective-permute-done.2.p3 = f32[8,256]{1,0:T(8,128)S(1)} collective-permute-done((f32[8,256]{1,0:T(8,128)S(1)}, f32[8,256]{1,0:T(8,128)S(1)}, u32[]{:S(2)}, u32[]{:S(2)}) %collective-permute-start.2) | collective-permute-done | bytes 8224 | tf_op jit(solution)/shard_map/ppermute | solution.py:446
  18.5 3.9 %shard_map.78 = (f32[8,128]{1,0:T(8,128)S(1)}, f32[8,128]{1,0:T(8,128)S(1)}, f32[8,256]{1,0:T(8,128)S(1)}) custom-call(s32[1]{0:T(128)S(6)} %copy.8.cnt, s32[16]{0:T(128)S(1)} %add_bitcast_fusion.pairs, s32[4]{0:T(128)S(1)} %pad_add_fusion.place, f32[16,256,256]{2,1,0:T(8,128)} %get-tuple-element.32.held, f32[8,256]{1,0:T(8,128)S(1)} %get-tuple-element.33.p0, ...), custom_call_target="tpu_custom_call" | custom-call | flops 16777216 | bytes 8388608 | tf_op jit(solution)/shard_map/pallas_call | solution.py:428
  22.5 1.2 collective-permute-done.3
  23.7 19.3 %all_to_all.20.mine = f32[32,8,128]{2,1,0:T(8,128)S(1)} all-to-all(f32[32,8,128]{2,1,0:T(8,128)S(1)} %broadcast_in_dim.6), channel_id=1, replica_groups=mesh['y'=4,'z'=8,'c'=2,'x'=4] {'y','z'}, dimensions={0} | all-to-all | bytes 262144 | tf_op jit(solution)/shard_map/all_to_all | solution.py:457
  43.0 1.3 collective-permute-done.4.other
  44.3 4.4 %shard_map.79 = (f32[16,256,256]{2,1,0:T(8,128)}, f32[8,256]{1,0:T(8,128)S(1)}) custom-call(s32[1]{0:T(128)S(6)} %copy.8.cnt, s32[16]{0:T(128)S(1)} %add_bitcast_fusion.pairs, s32[4]{0:T(128)S(1)} %pad_add_fusion.place, f32[16,256,256]{2,1,0:T(8,128)} %get-tuple-element.32.held, f32[32,8,128]{2,1,0:T(8,128)S(1)} %all_to_all.20.mine, ...), custom_call_target="tpu_custom_call" | custom-call | flops 16777216 | bytes 8388608 | tf_op jit(solution)/shard_map/pallas_call | solution.py:428
  48.8 3.2 %collective-permute-start.6 = (f32[8,256]{1,0:T(8,128)S(1)}, f32[8,256]{1,0:T(8,128)S(1)}, u32[]{:S(2)}, u32[]{:S(2)}) collective-permute-start(f32[8,256]{1,0:T(8,128)S(1)} %get-tuple-element.38.p0), channel_id=1, source_target_pairs={{0,3},{1,0},{2,1},{3,2},{4,7},{5,4},{6,5},{7,6},{8,11},{9,8},{10,9... | collective-permute-start | bytes 24584 | tf_op jit(solution)/shard_map/ppermute | solution.py:446
  52.0 0.9 collective-permute-start.7
  52.9 0.8 collective-permute-done.5.p1
  53.7 3.5 %collective-permute-done.7.p3 = f32[8,256]{1,0:T(8,128)S(1)} collective-permute-done((f32[8,256]{1,0:T(8,128)S(1)}, f32[8,256]{1,0:T(8,128)S(1)}, u32[]{:S(2)}, u32[]{:S(2)}) %collective-permute-start.7) | collective-permute-done | bytes 8224 | tf_op jit(solution)/shard_map/ppermute | solution.py:446
  57.2 2.9 %shard_map.80 = (f32[8,128]{1,0:T(8,128)S(1)}, f32[8,128]{1,0:T(8,128)S(1)}) custom-call(s32[1]{0:T(128)S(6)} %copy.8.cnt, s32[16]{0:T(128)S(1)} %add_bitcast_fusion.pairs, s32[4]{0:T(128)S(1)} %pad_add_fusion.place, f32[16,256,256]{2,1,0:T(8,128)} %get-tuple-element.37.held, f32[8,256]{1,0:T(8,128)S(1)} %get-tuple-element.38.p0, ...), custom_call_target="tpu_custom_call" | custom-call | flops 16777216 | bytes 8388608 | tf_op jit(solution)/shard_map/pallas_call | solution.py:428
  60.2 1.2 collective-permute-done.8
  61.4 13.9 %all_to_all.21.mine = f32[32,8,128]{2,1,0:T(8,128)S(1)} all-to-all(f32[32,8,128]{2,1,0:T(8,128)S(1)} %broadcast_in_dim.7), channel_id=1, replica_groups=mesh['y'=4,'z'=8,'c'=2,'x'=4] {'y','z'}, dimensions={0} | all-to-all | bytes 262144 | tf_op jit(solution)/shard_map/all_to_all | solution.py:457
  75.2 1.3 collective-permute-done.9.other
  76.6 3.2 %shard_map.81.p0 = f32[8,256]{1,0:T(8,128)S(1)} custom-call(s32[1]{0:T(128)S(6)} %copy.8.cnt, s32[16]{0:T(128)S(1)} %add_bitcast_fusion.pairs, s32[4]{0:T(128)S(1)} %pad_add_fusion.place, f32[16,256,256]{2,1,0:T(8,128)} %get-tuple-element.37.held, f32[32,8,128]{2,1,0:T(8,128)S(1)} %all_to_all.21.mine, f32[32,8,128]{2,1,0:T(8,128)S(1)} %collective-permute-done.9.other, ...), custom_call_target="tpu_custom_call" | custom-call | flops 16777216 | bytes 8388608 | tf_op jit(solution)/shard_map/pallas_call | solution.py:428
  79.9 3.2 %collective-permute-start.11 = (f32[8,256]{1,0:T(8,128)S(1)}, f32[8,256]{1,0:T(8,128)S(1)}, u32[]{:S(2)}, u32[]{:S(2)}) collective-permute-start(f32[8,256]{1,0:T(8,128)S(1)} %shard_map.81.p0), channel_id=1, source_target_pairs={{0,3},{1,0},{2,1},{3,2},{4,7},{5,4},{6,5},{7,6},{8,11},{9,8},{10,9... | collective-permute-start | bytes 24584 | tf_op jit(solution)/shard_map/ppermute | solution.py:446
  83.5 1.2 collective-permute-done.10.p1
  84.7 3.5 %collective-permute-done.12.p3 = f32[8,256]{1,0:T(8,128)S(1)} collective-permute-done((f32[8,256]{1,0:T(8,128)S(1)}, f32[8,256]{1,0:T(8,128)S(1)}, u32[]{:S(2)}, u32[]{:S(2)}) %collective-permute-start.12) | collective-permute-done | bytes 8224 | tf_op jit(solution)/shard_map/ppermute | solution.py:446
  88.3 9.8 %shard_map.82 = (f32[8,128]{1,0:T(8,128)S(1)}, f32[8,128]{1,0:T(8,128)S(1)}, f32[8,256]{1,0:T(8,128)S(1)}, f32[4,8,32,512]{3,2,1,0:T(8,128)S(1)}, f32[4,8,32,512]{3,2,1,0:T(8,128)}) custom-call(s32[1]{0:T(128)S(6)} %copy.8.cnt, s32[16]{0:T(128)S(1)} %add_bitcast_fusion.pairs, s32[4]{0:T(128)S(1)} %pad_add_fusion.place, ...), custom_call_target="tpu_custom_call" | custom-call | flops 2147483648 | bytes 8388608 | tf_op jit(solution)/shard_map/pallas_call | solution.py:428
  98.1 4.4 %collective-permute-done.21.got = f32[4,8,32,512]{3,2,1,0:T(8,128)S(1)} collective-permute-done((f32[4,8,32,512]{3,2,1,0:T(8,128)}, f32[4,8,32,512]{3,2,1,0:T(8,128)S(1)}, u32[]{:S(2)}, u32[]{:S(2)}) %collective-permute-start.21) | collective-permute-done | bytes 2097184 | tf_op jit(solution)/shard_map/ppermute | solution.py:446
  103.0 1.0 collective-permute-done.13
  104.1 0.7 broadcast_in_dim.8
  104.7 6.6 %all-to-all-start.2 = ((f32[32,8,128]{2,1,0:T(8,128)}), f32[32,8,128]{2,1,0:T(8,128)S(1)}, u32[]{:S(2)}, u32[]{:S(2)}) async-start(f32[32,8,128]{2,1,0:T(8,128)} %broadcast_in_dim.8), calls=%async_computation.2 | async-start | bytes 262144 | tf_op jit(solution)/shard_map/all_to_all | solution.py:457
  111.7 3.0 %collective-permute-start.24 = (f32[4,32,512]{2,1,0:T(8,128)S(1)}, f32[4,32,512]{2,1,0:T(8,128)}, u32[]{:S(2)}, u32[]{:S(2)}) collective-permute-start(f32[4,32,512]{2,1,0:T(8,128)S(1)} %get-tuple-element.57), channel_id=1, source_target_pairs={{0,192},{64,0},{128,64},{192,128},{1,193},{65,1},{129,65},{193,129... | collective-permute-start | bytes 786440 | tf_op jit(solution)/shard_map/ppermute | solution.py:446
  114.9 6.1 %all-to-all-done.2.mine = f32[32,8,128]{2,1,0:T(8,128)S(1)} async-done(((f32[32,8,128]{2,1,0:T(8,128)}), f32[32,8,128]{2,1,0:T(8,128)S(1)}, u32[]{:S(2)}, u32[]{:S(2)}) %all-to-all-start.2) | async-done | bytes 131104 | tf_op jit(solution)/shard_map/all_to_all | solution.py:457
  120.9 0.6 collective-permute-start.25
  121.9 1.2 collective-permute-start.27
  123.1 4.0 %shard_map.84 = (f32[264,512]{1,0:T(8,128)S(1)}, f32[264,512]{1,0:T(8,128)S(1)}) custom-call(s32[1]{0:T(128)S(6)} %copy.8.cnt, s32[16]{0:T(128)S(1)} %add_bitcast_fusion.pairs, s32[4]{0:T(128)S(1)} %pad_add_fusion.place, f32[16,256,256]{2,1,0:T(8,128)} %get-tuple-element.37.held, f32[32,8,128]{2,1,0:T(8,128)S(1)} %all-to-all-done.2.mine, ...), custom_call_target="tpu_custom_call" | custom-call | flops 536870912 | bytes 8388608 | tf_op jit(solution)/shard_map/pallas_call | solution.py:428
  127.6 1.6 collective-permute-start.15
  129.2 1.1 add_add_fusion.1
  130.3 1.5 collective-permute-done.27
  131.9 0.9 pad_maximum_fusion
  132.8 6.6 %all-to-all-start.3 = ((f32[8,32,512]{2,1,0:T(8,128)}), f32[8,32,512]{2,1,0:T(8,128)S(1)}, u32[]{:S(2)}, u32[]{:S(2)}) async-start(f32[8,32,512]{2,1,0:T(8,128)} %pad_maximum_fusion), calls=%async_computation.3 | async-start | bytes 1048576 | tf_op jit(solution)/shard_map/all_to_all | solution.py:577
  139.5 5.8 %shard_map.83 = (f32[264,512]{1,0:T(8,128)S(1)}, f32[264,512]{1,0:T(8,128)S(1)}, f32[264,512]{1,0:T(8,128)S(1)}, f32[264,512]{1,0:T(8,128)S(1)}, f32[264,512]{1,0:T(8,128)S(1)}, /*index=5*/f32[264,512]{1,0:T(8,128)}) custom-call(s32[1]{0:T(128)S(6)} %copy.8.cnt, s32[16]{0:T(128)S(1)} %add_bitcast_fusion.pairs, s32[4]{0:T(128)S(1)} %pad_add_fusion.place, ...), custom_call_target="tpu_custom_call" | custom-call | flops 536870912 | bytes 8388608 | tf_op jit(solution)/shard_map/pallas_call | solution.py:428
  145.7 1.6 collective-permute-start.18
  147.3 1.1 add.48
  148.5 1.7 collective-permute-start.20
  150.8 9.7 %collective-permute-done.17.refs_2_ = f32[264,512]{1,0:T(8,128)S(1)} collective-permute-done((f32[264,512]{1,0:T(8,128)S(1)}, f32[264,512]{1,0:T(8,128)S(1)}, u32[]{:S(2)}, u32[]{:S(2)}) %collective-permute-start.17) | collective-permute-done | bytes 540704 | tf_op jit(solution)/shard_map/ppermute | solution.py:446
  160.5 1.8 %collective-permute-done.18.refs_4_ = f32[264,512]{1,0:T(8,128)S(1)} collective-permute-done((f32[264,512]{1,0:T(8,128)}, f32[264,512]{1,0:T(8,128)S(1)}, u32[]{:S(2)}, u32[]{:S(2)}) %collective-permute-start.18) | collective-permute-done | bytes 540704 | tf_op jit(solution)/shard_map/ppermute | solution.py:446
  162.3 9.0 %collective-permute-done.20.refs_5_ = f32[264,512]{1,0:T(8,128)S(1)} collective-permute-done((f32[264,512]{1,0:T(8,128)S(1)}, f32[264,512]{1,0:T(8,128)S(1)}, u32[]{:S(2)}, u32[]{:S(2)}) %collective-permute-start.20) | collective-permute-done | bytes 540704 | tf_op jit(solution)/shard_map/ppermute | solution.py:446
  171.3 1.8 %collective-permute-done.16.refs_1_ = f32[264,512]{1,0:T(8,128)S(1)} collective-permute-done((f32[264,512]{1,0:T(8,128)S(1)}, f32[264,512]{1,0:T(8,128)S(1)}, u32[]{:S(2)}, u32[]{:S(2)}) %collective-permute-start.16) | collective-permute-done | bytes 540704 | tf_op jit(solution)/shard_map/ppermute | solution.py:446
  173.1 1.3 shard_map.85
  174.5 1.4 shard_map.87
  (46 shorter events, 4.0 us)
Async XLA Ops:
  2.0 12.4 %copy-start = (f32[2048]{0:T(1024)S(1)}, f32[2048]{0:T(1024)}, u32[]{:S(2)}) copy-start(f32[2048]{0:T(1024)} %param.8) | copy-start | bytes 24580
  10.0 4.9 %collective-permute-start = (f32[8,256]{1,0:T(8,128)S(1)}, f32[8,256]{1,0:T(8,128)S(1)}, u32[]{:S(2)}, u32[]{:S(2)}) collective-permute-start(f32[8,256]{1,0:T(8,128)S(1)} %get-tuple-element.33.p0), channel_id=1, source_target_pairs={{0,1},{1,2},{2,3},{3,0},{4,5},{5,6},{6,7},{7,4},{8,9},{9,10},{10,1... | collective-permute-start | bytes 24584 | tf_op jit(solution)/shard_map/ppermute | solution.py:446
  10.1 4.9 %collective-permute-start.1 = (f32[8,256]{1,0:T(8,128)S(1)}, f32[8,256]{1,0:T(8,128)S(1)}, u32[]{:S(2)}, u32[]{:S(2)}) collective-permute-start(f32[8,256]{1,0:T(8,128)S(1)} %get-tuple-element.33.p0), channel_id=1, source_target_pairs={{0,3},{1,0},{2,1},{3,2},{4,7},{5,4},{6,5},{7,6},{8,11},{9,8},{10,9... | collective-permute-start | bytes 24584 | tf_op jit(solution)/shard_map/ppermute | solution.py:446
  13.3 5.2 %collective-permute-start.2 = (f32[8,256]{1,0:T(8,128)S(1)}, f32[8,256]{1,0:T(8,128)S(1)}, u32[]{:S(2)}, u32[]{:S(2)}) collective-permute-start(f32[8,256]{1,0:T(8,128)S(1)} %get-tuple-element.33.p0), channel_id=1, source_target_pairs={{0,2},{1,3},{2,0},{3,1},{4,6},{5,7},{6,4},{7,5},{8,10},{9,11},{10,... | collective-permute-start | bytes 24584 | tf_op jit(solution)/shard_map/ppermute | solution.py:446
  18.5 24.5 %copy-start.1 = (f32[2048]{0:T(1024)S(1)}, f32[2048]{0:T(1024)}, u32[]{:S(2)}) copy-start(f32[2048]{0:T(1024)} %param.9) | copy-start | bytes 24580
  22.4 1.3 collective-permute-start.3
  43.0 1.3 collective-permute-start.4
  48.7 4.9 %collective-permute-start.5 = (f32[8,256]{1,0:T(8,128)S(1)}, f32[8,256]{1,0:T(8,128)S(1)}, u32[]{:S(2)}, u32[]{:S(2)}) collective-permute-start(f32[8,256]{1,0:T(8,128)S(1)} %get-tuple-element.38.p0), channel_id=1, source_target_pairs={{0,1},{1,2},{2,3},{3,0},{4,5},{5,6},{6,7},{7,4},{8,9},{9,10},{10,1... | collective-permute-start | bytes 24584 | tf_op jit(solution)/shard_map/ppermute | solution.py:446
  48.8 4.9 %collective-permute-start.6 = (f32[8,256]{1,0:T(8,128)S(1)}, f32[8,256]{1,0:T(8,128)S(1)}, u32[]{:S(2)}, u32[]{:S(2)}) collective-permute-start(f32[8,256]{1,0:T(8,128)S(1)} %get-tuple-element.38.p0), channel_id=1, source_target_pairs={{0,3},{1,0},{2,1},{3,2},{4,7},{5,4},{6,5},{7,6},{8,11},{9,8},{10,9... | collective-permute-start | bytes 24584 | tf_op jit(solution)/shard_map/ppermute | solution.py:446
  52.0 5.2 %collective-permute-start.7 = (f32[8,256]{1,0:T(8,128)S(1)}, f32[8,256]{1,0:T(8,128)S(1)}, u32[]{:S(2)}, u32[]{:S(2)}) collective-permute-start(f32[8,256]{1,0:T(8,128)S(1)} %get-tuple-element.38.p0), channel_id=1, source_target_pairs={{0,2},{1,3},{2,0},{3,1},{4,6},{5,7},{6,4},{7,5},{8,10},{9,11},{10,... | collective-permute-start | bytes 24584 | tf_op jit(solution)/shard_map/ppermute | solution.py:446
  60.1 1.3 collective-permute-start.8
  75.2 1.3 collective-permute-start.9
  79.8 4.9 %collective-permute-start.10 = (f32[8,256]{1,0:T(8,128)S(1)}, f32[8,256]{1,0:T(8,128)S(1)}, u32[]{:S(2)}, u32[]{:S(2)}) collective-permute-start(f32[8,256]{1,0:T(8,128)S(1)} %shard_map.81.p0), channel_id=1, source_target_pairs={{0,1},{1,2},{2,3},{3,0},{4,5},{5,6},{6,7},{7,4},{8,9},{9,10},{10,1... | collective-permute-start | bytes 24584 | tf_op jit(solution)/shard_map/ppermute | solution.py:446
  79.9 4.9 %collective-permute-start.11 = (f32[8,256]{1,0:T(8,128)S(1)}, f32[8,256]{1,0:T(8,128)S(1)}, u32[]{:S(2)}, u32[]{:S(2)}) collective-permute-start(f32[8,256]{1,0:T(8,128)S(1)} %shard_map.81.p0), channel_id=1, source_target_pairs={{0,3},{1,0},{2,1},{3,2},{4,7},{5,4},{6,5},{7,6},{8,11},{9,8},{10,9... | collective-permute-start | bytes 24584 | tf_op jit(solution)/shard_map/ppermute | solution.py:446
  83.1 5.2 %collective-permute-start.12 = (f32[8,256]{1,0:T(8,128)S(1)}, f32[8,256]{1,0:T(8,128)S(1)}, u32[]{:S(2)}, u32[]{:S(2)}) collective-permute-start(f32[8,256]{1,0:T(8,128)S(1)} %shard_map.81.p0), channel_id=1, source_target_pairs={{0,2},{1,3},{2,0},{3,1},{4,6},{5,7},{6,4},{7,5},{8,10},{9,11},{10,... | collective-permute-start | bytes 24584 | tf_op jit(solution)/shard_map/ppermute | solution.py:446
  98.0 4.5 %collective-permute-start.21 = (f32[4,8,32,512]{3,2,1,0:T(8,128)}, f32[4,8,32,512]{3,2,1,0:T(8,128)S(1)}, u32[]{:S(2)}, u32[]{:S(2)}) collective-permute-start(f32[4,8,32,512]{3,2,1,0:T(8,128)} %get-tuple-element.53), channel_id=1, source_target_pairs={{0,4},{4,0},{1,5},{5,1},{2,6},{6,2},{3,7},{7,3},{8,12},{12,8},{9,1... | collective-permute-start | bytes 6291464 | tf_op jit(solution)/shard_map/ppermute | solution.py:446
  102.7 12.0 %collective-permute-start.22 = (f32[4,32,512]{2,1,0:T(8,128)S(1)}, f32[4,32,512]{2,1,0:T(8,128)S(1)}, u32[]{:S(2)}, u32[]{:S(2)}) collective-permute-start(f32[4,32,512]{2,1,0:T(8,128)S(1)} %get-tuple-element.56), channel_id=1, source_target_pairs={{0,64},{64,128},{128,192},{192,0},{1,65},{65,129},{129,193},{193,1... | collective-permute-start | bytes 786440 | tf_op jit(solution)/shard_map/ppermute | solution.py:446
  102.8 1.3 collective-permute-start.13
  104.7 16.2 %all-to-all-start.2 = ((f32[32,8,128]{2,1,0:T(8,128)}), f32[32,8,128]{2,1,0:T(8,128)S(1)}, u32[]{:S(2)}, u32[]{:S(2)}) async-start(f32[32,8,128]{2,1,0:T(8,128)} %broadcast_in_dim.8), calls=%async_computation.2 | async-start | bytes 262144 | tf_op jit(solution)/shard_map/all_to_all | solution.py:457
  111.4 10.5 %collective-permute-start.26 = (f32[4,32,512]{2,1,0:T(8,128)S(1)}, f32[4,32,512]{2,1,0:T(8,128)S(1)}, u32[]{:S(2)}, u32[]{:S(2)}) collective-permute-start(f32[4,32,512]{2,1,0:T(8,128)S(1)} %get-tuple-element.61), channel_id=1, source_target_pairs={{0,192},{64,0},{128,64},{192,128},{1,193},{65,1},{129,65},{193,129... | collective-permute-start | bytes 786440 | tf_op jit(solution)/shard_map/ppermute | solution.py:446
  111.7 15.9 %collective-permute-start.24 = (f32[4,32,512]{2,1,0:T(8,128)S(1)}, f32[4,32,512]{2,1,0:T(8,128)}, u32[]{:S(2)}, u32[]{:S(2)}) collective-permute-start(f32[4,32,512]{2,1,0:T(8,128)S(1)} %get-tuple-element.57), channel_id=1, source_target_pairs={{0,192},{64,0},{128,64},{192,128},{1,193},{65,1},{129,65},{193,129... | collective-permute-start | bytes 786440 | tf_op jit(solution)/shard_map/ppermute | solution.py:446
  114.8 14.4 %collective-permute-start.23 = (f32[4,32,512]{2,1,0:T(8,128)S(1)}, f32[4,32,512]{2,1,0:T(8,128)}, u32[]{:S(2)}, u32[]{:S(2)}) collective-permute-start(f32[4,32,512]{2,1,0:T(8,128)S(1)} %add.49), channel_id=1, source_target_pairs={{0,64},{64,128},{128,192},{192,0},{1,65},{65,129},{129,193},{193,1... | collective-permute-start | bytes 786440 | tf_op jit(solution)/shard_map/ppermute | solution.py:446
  120.9 2.2 %collective-permute-start.14 = (f32[32,8,128]{2,1,0:T(8,128)S(1)}, f32[32,8,128]{2,1,0:T(8,128)S(1)}, u32[]{:S(2)}, u32[]{:S(2)}) collective-permute-start(f32[32,8,128]{2,1,0:T(8,128)S(1)} %all-to-all-done.2.mine), channel_id=1, source_target_pairs={{0,4},{4,0},{1,5},{5,1},{2,6},{6,2},{3,7},{7,3},{8,12},{12,8},{9,1... | collective-permute-start | bytes 393224 | tf_op jit(solution)/shard_map/ppermute | solution.py:446
  120.9 9.4 %collective-permute-start.25 = (f32[4,32,512]{2,1,0:T(8,128)S(1)}, f32[4,32,512]{2,1,0:T(8,128)S(1)}, u32[]{:S(2)}, u32[]{:S(2)}) collective-permute-start(f32[4,32,512]{2,1,0:T(8,128)S(1)} %get-tuple-element.59), channel_id=1, source_target_pairs={{0,64},{64,128},{128,192},{192,0},{1,65},{65,129},{129,193},{193,1... | collective-permute-start | bytes 786440 | tf_op jit(solution)/shard_map/ppermute | solution.py:446
  121.9 10.0 %collective-permute-start.27 = (f32[4,32,512]{2,1,0:T(8,128)S(1)}, f32[4,32,512]{2,1,0:T(8,128)S(1)}, u32[]{:S(2)}, u32[]{:S(2)}) collective-permute-start(f32[4,32,512]{2,1,0:T(8,128)S(1)} %add.53), channel_id=1, source_target_pairs={{0,192},{64,0},{128,64},{192,128},{1,193},{65,1},{129,65},{193,129... | collective-permute-start | bytes 786440 | tf_op jit(solution)/shard_map/ppermute | solution.py:446
  127.1 20.2 %collective-permute-start.19 = (f32[264,512]{1,0:T(8,128)S(1)}, f32[264,512]{1,0:T(8,128)}, u32[]{:S(2)}, u32[]{:S(2)}) collective-permute-start(f32[264,512]{1,0:T(8,128)S(1)} %get-tuple-element.51), channel_id=1, source_target_pairs={{0,3},{1,0},{2,1},{3,2},{4,7},{5,4},{6,5},{7,6},{8,11},{9,8},{10,9... | collective-permute-start | bytes 1622024 | tf_op jit(solution)/shard_map/ppermute | solution.py:446
  127.6 22.6 %collective-permute-start.15 = (f32[264,512]{1,0:T(8,128)S(1)}, f32[264,512]{1,0:T(8,128)S(1)}, u32[]{:S(2)}, u32[]{:S(2)}) collective-permute-start(f32[264,512]{1,0:T(8,128)S(1)} %get-tuple-element.46), channel_id=1, source_target_pairs={{0,1},{1,2},{2,3},{3,0},{4,5},{5,6},{6,7},{7,4},{8,9},{9,10},{10,1... | collective-permute-start | bytes 1622024 | tf_op jit(solution)/shard_map/ppermute | solution.py:446
  132.8 41.6 %all-to-all-start.3 = ((f32[8,32,512]{2,1,0:T(8,128)}), f32[8,32,512]{2,1,0:T(8,128)S(1)}, u32[]{:S(2)}, u32[]{:S(2)}) async-start(f32[8,32,512]{2,1,0:T(8,128)} %pad_maximum_fusion), calls=%async_computation.3 | async-start | bytes 1048576 | tf_op jit(solution)/shard_map/all_to_all | solution.py:577
  145.2 15.2 %collective-permute-start.17 = (f32[264,512]{1,0:T(8,128)S(1)}, f32[264,512]{1,0:T(8,128)S(1)}, u32[]{:S(2)}, u32[]{:S(2)}) collective-permute-start(f32[264,512]{1,0:T(8,128)S(1)} %get-tuple-element.47), channel_id=1, source_target_pairs={{0,3},{1,0},{2,1},{3,2},{4,7},{5,4},{6,5},{7,6},{8,11},{9,8},{10,9... | collective-permute-start | bytes 1622024 | tf_op jit(solution)/shard_map/ppermute | solution.py:446
  145.7 16.6 %collective-permute-start.18 = (f32[264,512]{1,0:T(8,128)}, f32[264,512]{1,0:T(8,128)S(1)}, u32[]{:S(2)}, u32[]{:S(2)}) collective-permute-start(f32[264,512]{1,0:T(8,128)} %get-tuple-element.49), channel_id=1, source_target_pairs={{0,1},{1,2},{2,3},{3,0},{4,5},{5,6},{6,7},{7,4},{8,9},{9,10},{10,1... | collective-permute-start | bytes 1622024 | tf_op jit(solution)/shard_map/ppermute | solution.py:446
  148.5 22.8 %collective-permute-start.20 = (f32[264,512]{1,0:T(8,128)S(1)}, f32[264,512]{1,0:T(8,128)S(1)}, u32[]{:S(2)}, u32[]{:S(2)}) collective-permute-start(f32[264,512]{1,0:T(8,128)S(1)} %add.48), channel_id=1, source_target_pairs={{0,3},{1,0},{2,1},{3,2},{4,7},{5,4},{6,5},{7,6},{8,11},{9,8},{10,9... | collective-permute-start | bytes 1622024 | tf_op jit(solution)/shard_map/ppermute | solution.py:446
  150.2 22.9 %collective-permute-start.16 = (f32[264,512]{1,0:T(8,128)S(1)}, f32[264,512]{1,0:T(8,128)S(1)}, u32[]{:S(2)}, u32[]{:S(2)}) collective-permute-start(f32[264,512]{1,0:T(8,128)S(1)} %add.47), channel_id=1, source_target_pairs={{0,1},{1,2},{2,3},{3,0},{4,5},{5,6},{6,7},{7,4},{8,9},{9,10},{10,1... | collective-permute-start | bytes 1622024 | tf_op jit(solution)/shard_map/ppermute | solution.py:446

commit v3 on v2

--- a/solution.py
+++ b/solution.py
@@ -138,6 +138,9 @@
         copy.wait()
 
     last = cnt[0] - 1
+
+    def send_out(k):
+        pltpu.make_async_copy(scores.at[k], held.at[k], sem.at[k]).start()
 
     def two(i, _):
         picks = []
@@ -151,10 +154,15 @@
         for k, a, tile in picks:
             scores[k] = tile
             m_ref[a] = jnp.maximum(m_ref[a], jnp.maximum(tile[:, :128], tile[:, 128:]))
+        send_out(2 * i)
+
+        @pl.when(2 * i < last)
+        def _():
+            send_out(2 * i + 1)
+
         return 0
 
     lax.fori_loop(0, (cnt[0] + 1) // 2, two, 0)
-    every_slot(cnt, lambda k: pltpu.make_async_copy(scores.at[k], held.at[k], sem.at[k]).start())
     row_totals(cnt, pairs, scores, None, m_ref, s_ref, lse_out)
     every_slot(cnt, lambda k: pltpu.make_async_copy(scores.at[k], held.at[k], sem.at[k]).wait())
 

time: 176 us -> 176 us (level)
  no operation moved by 1% of the time
where the time goes in v3:
time: 176 us; the launch traced here: 175 us
  waiting for transfers between devices  54.1 us (31%)
  Pallas kernels  44.5 us (25%)
  starting transfers between devices  37.3 us (21%)
  blocking collectives  33.1 us (19%)
  other arithmetic  4.18 us (2%)
    ppermute x28, waiting for transfers between devices, shift(): return lax.ppermute(a, axis, [(i, (i + by) % size) for i in range(size)])  48.1 us
    pallas_call x11, Pallas kernels, call(): pl.pallas_call(kernel, out_shape=outs, in_specs=specs, out_specs=out_spec...  44.5 us
    all_to_all x2, blocking collectives, over_src(): stack = lax.all_to_all(copies, ('y', 'z'), 0, 0, tiled=True)  33.1 us
    ppermute x28, starting transfers between devices, shift(): return lax.ppermute(a, axis, [(i, (i + by) % size) for i in range(size)])  24.1 us
    all_to_all x1, starting transfers between devices, program(): got = lax.all_to_all(summed, 'z', 0, 0, tiled=True)  6.65 us
    all_to_all x1, starting transfers between devices, over_src(): stack = lax.all_to_all(copies, ('y', 'z'), 0, 0, tiled=True)  6.62 us
    all_to_all x1, waiting for transfers between devices, over_src(): stack = lax.all_to_all(copies, ('y', 'z'), 0, 0, tiled=True)  6.07 us
  transfers between devices with their start and end apart: 30, of which 20 were waited for; matrix products, arithmetic and copies ran while one was open for 2% of the time, Pallas kernels for 6%

profile of v3, /device:TPU:8, one launch (start us, length us, event | category | flops | bytes accessed | tf_op | source)
XLA Modules:
  0.0 175.5 jit_solution(17916248888385820246)
XLA Ops:
  0.6 0.8 add_bitcast_fusion.pairs
  2.1 7.5 %shard_map.77 = (f32[16,256,256]{2,1,0:T(8,128)}, f32[8,256]{1,0:T(8,128)S(1)}) custom-call(s32[1]{0:T(128)S(6)} %copy.8.cnt, s32[16]{0:T(128)S(1)} %add_bitcast_fusion.pairs, bf16[2048,512]{1,0:T(8,128)(2,1)} %text.3, bf16[2048,512]{1,0:T(8,128)(2,1)} %image.5), custom_call_target="tpu_custom_call" | custom-call | flops 1073741824 | bytes 8388608 | tf_op jit(solution)/shard_map/pallas_call | solution.py:436
  9.7 3.2 %collective-permute-start.1 = (f32[8,256]{1,0:T(8,128)S(1)}, f32[8,256]{1,0:T(8,128)S(1)}, u32[]{:S(2)}, u32[]{:S(2)}) collective-permute-start(f32[8,256]{1,0:T(8,128)S(1)} %get-tuple-element.33.p0), channel_id=1, source_target_pairs={{0,3},{1,0},{2,1},{3,2},{4,7},{5,4},{6,5},{7,6},{8,11},{9,8},{10,9... | collective-permute-start | bytes 24584 | tf_op jit(solution)/shard_map/ppermute | solution.py:454
  12.9 1.0 collective-permute-start.2
  14.0 0.6 collective-permute-done.p1
  14.6 3.5 %collective-permute-done.2.p3 = f32[8,256]{1,0:T(8,128)S(1)} collective-permute-done((f32[8,256]{1,0:T(8,128)S(1)}, f32[8,256]{1,0:T(8,128)S(1)}, u32[]{:S(2)}, u32[]{:S(2)}) %collective-permute-start.2) | collective-permute-done | bytes 8224 | tf_op jit(solution)/shard_map/ppermute | solution.py:454
  18.1 3.9 %shard_map.78 = (f32[8,128]{1,0:T(8,128)S(1)}, f32[8,128]{1,0:T(8,128)S(1)}, f32[8,256]{1,0:T(8,128)S(1)}) custom-call(s32[1]{0:T(128)S(6)} %copy.8.cnt, s32[16]{0:T(128)S(1)} %add_bitcast_fusion.pairs, s32[4]{0:T(128)S(1)} %pad_add_fusion.place, f32[16,256,256]{2,1,0:T(8,128)} %get-tuple-element.32.held, f32[8,256]{1,0:T(8,128)S(1)} %get-tuple-element.33.p0, ...), custom_call_target="tpu_custom_call" | custom-call | flops 16777216 | bytes 8388608 | tf_op jit(solution)/shard_map/pallas_call | solution.py:436
  22.1 1.2 collective-permute-done.3
  23.3 19.3 %all_to_all.20.mine = f32[32,8,128]{2,1,0:T(8,128)S(1)} all-to-all(f32[32,8,128]{2,1,0:T(8,128)S(1)} %broadcast_in_dim.6), channel_id=1, replica_groups=mesh['y'=4,'z'=8,'c'=2,'x'=4] {'y','z'}, dimensions={0} | all-to-all | bytes 262144 | tf_op jit(solution)/shard_map/all_to_all | solution.py:465
  42.6 1.3 collective-permute-done.4.other
  43.9 4.4 %shard_map.79 = (f32[16,256,256]{2,1,0:T(8,128)}, f32[8,256]{1,0:T(8,128)S(1)}) custom-call(s32[1]{0:T(128)S(6)} %copy.8.cnt, s32[16]{0:T(128)S(1)} %add_bitcast_fusion.pairs, s32[4]{0:T(128)S(1)} %pad_add_fusion.place, f32[16,256,256]{2,1,0:T(8,128)} %get-tuple-element.32.held, f32[32,8,128]{2,1,0:T(8,128)S(1)} %all_to_all.20.mine, ...), custom_call_target="tpu_custom_call" | custom-call | flops 16777216 | bytes 8388608 | tf_op jit(solution)/shard_map/pallas_call | solution.py:436
  48.4 3.2 %collective-permute-start.6 = (f32[8,256]{1,0:T(8,128)S(1)}, f32[8,256]{1,0:T(8,128)S(1)}, u32[]{:S(2)}, u32[]{:S(2)}) collective-permute-start(f32[8,256]{1,0:T(8,128)S(1)} %get-tuple-element.38.p0), channel_id=1, source_target_pairs={{0,3},{1,0},{2,1},{3,2},{4,7},{5,4},{6,5},{7,6},{8,11},{9,8},{10,9... | collective-permute-start | bytes 24584 | tf_op jit(solution)/shard_map/ppermute | solution.py:454
  51.6 0.9 collective-permute-start.7
  52.5 0.8 collective-permute-done.5.p1
  53.2 3.5 %collective-permute-done.7.p3 = f32[8,256]{1,0:T(8,128)S(1)} collective-permute-done((f32[8,256]{1,0:T(8,128)S(1)}, f32[8,256]{1,0:T(8,128)S(1)}, u32[]{:S(2)}, u32[]{:S(2)}) %collective-permute-start.7) | collective-permute-done | bytes 8224 | tf_op jit(solution)/shard_map/ppermute | solution.py:454
  56.8 2.9 %shard_map.80 = (f32[8,128]{1,0:T(8,128)S(1)}, f32[8,128]{1,0:T(8,128)S(1)}) custom-call(s32[1]{0:T(128)S(6)} %copy.8.cnt, s32[16]{0:T(128)S(1)} %add_bitcast_fusion.pairs, s32[4]{0:T(128)S(1)} %pad_add_fusion.place, f32[16,256,256]{2,1,0:T(8,128)} %get-tuple-element.37.held, f32[8,256]{1,0:T(8,128)S(1)} %get-tuple-element.38.p0, ...), custom_call_target="tpu_custom_call" | custom-call | flops 16777216 | bytes 8388608 | tf_op jit(solution)/shard_map/pallas_call | solution.py:436
  59.8 1.2 collective-permute-done.8
  60.9 13.9 %all_to_all.21.mine = f32[32,8,128]{2,1,0:T(8,128)S(1)} all-to-all(f32[32,8,128]{2,1,0:T(8,128)S(1)} %broadcast_in_dim.7), channel_id=1, replica_groups=mesh['y'=4,'z'=8,'c'=2,'x'=4] {'y','z'}, dimensions={0} | all-to-all | bytes 262144 | tf_op jit(solution)/shard_map/all_to_all | solution.py:465
  74.8 1.3 collective-permute-done.9.other
  76.2 3.2 %shard_map.81.p0 = f32[8,256]{1,0:T(8,128)S(1)} custom-call(s32[1]{0:T(128)S(6)} %copy.8.cnt, s32[16]{0:T(128)S(1)} %add_bitcast_fusion.pairs, s32[4]{0:T(128)S(1)} %pad_add_fusion.place, f32[16,256,256]{2,1,0:T(8,128)} %get-tuple-element.37.held, f32[32,8,128]{2,1,0:T(8,128)S(1)} %all_to_all.21.mine, f32[32,8,128]{2,1,0:T(8,128)S(1)} %collective-permute-done.9.other, ...), custom_call_target="tpu_custom_call" | custom-call | flops 16777216 | bytes 8388608 | tf_op jit(solution)/shard_map/pallas_call | solution.py:436
  79.5 3.2 %collective-permute-start.11 = (f32[8,256]{1,0:T(8,128)S(1)}, f32[8,256]{1,0:T(8,128)S(1)}, u32[]{:S(2)}, u32[]{:S(2)}) collective-permute-start(f32[8,256]{1,0:T(8,128)S(1)} %shard_map.81.p0), channel_id=1, source_target_pairs={{0,3},{1,0},{2,1},{3,2},{4,7},{5,4},{6,5},{7,6},{8,11},{9,8},{10,9... | collective-permute-start | bytes 24584 | tf_op jit(solution)/shard_map/ppermute | solution.py:454
  83.1 1.2 collective-permute-done.10.p1
  84.3 3.5 %collective-permute-done.12.p3 = f32[8,256]{1,0:T(8,128)S(1)} collective-permute-done((f32[8,256]{1,0:T(8,128)S(1)}, f32[8,256]{1,0:T(8,128)S(1)}, u32[]{:S(2)}, u32[]{:S(2)}) %collective-permute-start.12) | collective-permute-done | bytes 8224 | tf_op jit(solution)/shard_map/ppermute | solution.py:454
  87.8 9.8 %shard_map.82 = (f32[8,128]{1,0:T(8,128)S(1)}, f32[8,128]{1,0:T(8,128)S(1)}, f32[8,256]{1,0:T(8,128)S(1)}, f32[4,8,32,512]{3,2,1,0:T(8,128)S(1)}, f32[4,8,32,512]{3,2,1,0:T(8,128)}) custom-call(s32[1]{0:T(128)S(6)} %copy.8.cnt, s32[16]{0:T(128)S(1)} %add_bitcast_fusion.pairs, s32[4]{0:T(128)S(1)} %pad_add_fusion.place, ...), custom_call_target="tpu_custom_call" | custom-call | flops 2147483648 | bytes 8388608 | tf_op jit(solution)/shard_map/pallas_call | solution.py:436
  97.7 4.4 %collective-permute-done.21.got = f32[4,8,32,512]{3,2,1,0:T(8,128)S(1)} collective-permute-done((f32[4,8,32,512]{3,2,1,0:T(8,128)}, f32[4,8,32,512]{3,2,1,0:T(8,128)S(1)}, u32[]{:S(2)}, u32[]{:S(2)}) %collective-permute-start.21) | collective-permute-done | bytes 2097184 | tf_op jit(solution)/shard_map/ppermute | solution.py:454
  102.6 1.0 collective-permute-done.13
  103.6 0.7 broadcast_in_dim.8
  104.3 6.6 %all-to-all-start.2 = ((f32[32,8,128]{2,1,0:T(8,128)}), f32[32,8,128]{2,1,0:T(8,128)S(1)}, u32[]{:S(2)}, u32[]{:S(2)}) async-start(f32[32,8,128]{2,1,0:T(8,128)} %broadcast_in_dim.8), calls=%async_computation.2 | async-start | bytes 262144 | tf_op jit(solution)/shard_map/all_to_all | solution.py:465
  111.2 3.0 %collective-permute-start.24 = (f32[4,32,512]{2,1,0:T(8,128)S(1)}, f32[4,32,512]{2,1,0:T(8,128)}, u32[]{:S(2)}, u32[]{:S(2)}) collective-permute-start(f32[4,32,512]{2,1,0:T(8,128)S(1)} %get-tuple-element.57), channel_id=1, source_target_pairs={{0,192},{64,0},{128,64},{192,128},{1,193},{65,1},{129,65},{193,129... | collective-permute-start | bytes 786440 | tf_op jit(solution)/shard_map/ppermute | solution.py:454
  114.4 6.1 %all-to-all-done.2.mine = f32[32,8,128]{2,1,0:T(8,128)S(1)} async-done(((f32[32,8,128]{2,1,0:T(8,128)}), f32[32,8,128]{2,1,0:T(8,128)S(1)}, u32[]{:S(2)}, u32[]{:S(2)}) %all-to-all-start.2) | async-done | bytes 131104 | tf_op jit(solution)/shard_map/all_to_all | solution.py:465
  120.5 0.6 collective-permute-start.25
  121.5 1.2 collective-permute-start.27
  122.7 4.0 %shard_map.84 = (f32[264,512]{1,0:T(8,128)S(1)}, f32[264,512]{1,0:T(8,128)S(1)}) custom-call(s32[1]{0:T(128)S(6)} %copy.8.cnt, s32[16]{0:T(128)S(1)} %add_bitcast_fusion.pairs, s32[4]{0:T(128)S(1)} %pad_add_fusion.place, f32[16,256,256]{2,1,0:T(8,128)} %get-tuple-element.37.held, f32[32,8,128]{2,1,0:T(8,128)S(1)} %all-to-all-done.2.mine, ...), custom_call_target="tpu_custom_call" | custom-call | flops 536870912 | bytes 8388608 | tf_op jit(solution)/shard_map/pallas_call | solution.py:436
  127.1 1.6 collective-permute-start.15
  128.8 1.1 add_add_fusion.1
  129.9 1.5 collective-permute-done.27
  131.5 0.9 pad_maximum_fusion
  132.4 6.6 %all-to-all-start.3 = ((f32[8,32,512]{2,1,0:T(8,128)}), f32[8,32,512]{2,1,0:T(8,128)S(1)}, u32[]{:S(2)}, u32[]{:S(2)}) async-start(f32[8,32,512]{2,1,0:T(8,128)} %pad_maximum_fusion), calls=%async_computation.3 | async-start | bytes 1048576 | tf_op jit(solution)/shard_map/all_to_all | solution.py:585
  139.0 5.8 %shard_map.83 = (f32[264,512]{1,0:T(8,128)S(1)}, f32[264,512]{1,0:T(8,128)S(1)}, f32[264,512]{1,0:T(8,128)S(1)}, f32[264,512]{1,0:T(8,128)S(1)}, f32[264,512]{1,0:T(8,128)S(1)}, /*index=5*/f32[264,512]{1,0:T(8,128)}) custom-call(s32[1]{0:T(128)S(6)} %copy.8.cnt, s32[16]{0:T(128)S(1)} %add_bitcast_fusion.pairs, s32[4]{0:T(128)S(1)} %pad_add_fusion.place, ...), custom_call_target="tpu_custom_call" | custom-call | flops 536870912 | bytes 8388608 | tf_op jit(solution)/shard_map/pallas_call | solution.py:436
  145.3 1.6 collective-permute-start.18
  146.9 1.1 add.48
  148.1 1.7 collective-permute-start.20
  150.3 9.7 %collective-permute-done.17.refs_2_ = f32[264,512]{1,0:T(8,128)S(1)} collective-permute-done((f32[264,512]{1,0:T(8,128)S(1)}, f32[264,512]{1,0:T(8,128)S(1)}, u32[]{:S(2)}, u32[]{:S(2)}) %collective-permute-start.17) | collective-permute-done | bytes 540704 | tf_op jit(solution)/shard_map/ppermute | solution.py:454
  160.0 1.8 %collective-permute-done.18.refs_4_ = f32[264,512]{1,0:T(8,128)S(1)} collective-permute-done((f32[264,512]{1,0:T(8,128)}, f32[264,512]{1,0:T(8,128)S(1)}, u32[]{:S(2)}, u32[]{:S(2)}) %collective-permute-start.18) | collective-permute-done | bytes 540704 | tf_op jit(solution)/shard_map/ppermute | solution.py:454
  161.9 9.0 %collective-permute-done.20.refs_5_ = f32[264,512]{1,0:T(8,128)S(1)} collective-permute-done((f32[264,512]{1,0:T(8,128)S(1)}, f32[264,512]{1,0:T(8,128)S(1)}, u32[]{:S(2)}, u32[]{:S(2)}) %collective-permute-start.20) | collective-permute-done | bytes 540704 | tf_op jit(solution)/shard_map/ppermute | solution.py:454
  170.9 1.8 %collective-permute-done.16.refs_1_ = f32[264,512]{1,0:T(8,128)S(1)} collective-permute-done((f32[264,512]{1,0:T(8,128)S(1)}, f32[264,512]{1,0:T(8,128)S(1)}, u32[]{:S(2)}, u32[]{:S(2)}) %collective-permute-start.16) | collective-permute-done | bytes 540704 | tf_op jit(solution)/shard_map/ppermute | solution.py:454
  172.7 1.3 shard_map.85
  174.0 1.4 shard_map.87
  (46 shorter events, 4.0 us)
Async XLA Ops:
  2.0 11.9 %copy-start = (f32[2048]{0:T(1024)S(1)}, f32[2048]{0:T(1024)}, u32[]{:S(2)}) copy-start(f32[2048]{0:T(1024)} %param.8) | copy-start | bytes 24580
  9.6 4.9 %collective-permute-start = (f32[8,256]{1,0:T(8,128)S(1)}, f32[8,256]{1,0:T(8,128)S(1)}, u32[]{:S(2)}, u32[]{:S(2)}) collective-permute-start(f32[8,256]{1,0:T(8,128)S(1)} %get-tuple-element.33.p0), channel_id=1, source_target_pairs={{0,1},{1,2},{2,3},{3,0},{4,5},{5,6},{6,7},{7,4},{8,9},{9,10},{10,1... | collective-permute-start | bytes 24584 | tf_op jit(solution)/shard_map/ppermute | solution.py:454
  9.7 4.9 %collective-permute-start.1 = (f32[8,256]{1,0:T(8,128)S(1)}, f32[8,256]{1,0:T(8,128)S(1)}, u32[]{:S(2)}, u32[]{:S(2)}) collective-permute-start(f32[8,256]{1,0:T(8,128)S(1)} %get-tuple-element.33.p0), channel_id=1, source_target_pairs={{0,3},{1,0},{2,1},{3,2},{4,7},{5,4},{6,5},{7,6},{8,11},{9,8},{10,9... | collective-permute-start | bytes 24584 | tf_op jit(solution)/shard_map/ppermute | solution.py:454
  12.9 5.2 %collective-permute-start.2 = (f32[8,256]{1,0:T(8,128)S(1)}, f32[8,256]{1,0:T(8,128)S(1)}, u32[]{:S(2)}, u32[]{:S(2)}) collective-permute-start(f32[8,256]{1,0:T(8,128)S(1)} %get-tuple-element.33.p0), channel_id=1, source_target_pairs={{0,2},{1,3},{2,0},{3,1},{4,6},{5,7},{6,4},{7,5},{8,10},{9,11},{10,... | collective-permute-start | bytes 24584 | tf_op jit(solution)/shard_map/ppermute | solution.py:454
  18.1 24.5 %copy-start.1 = (f32[2048]{0:T(1024)S(1)}, f32[2048]{0:T(1024)}, u32[]{:S(2)}) copy-start(f32[2048]{0:T(1024)} %param.9) | copy-start | bytes 24580
  22.0 1.3 collective-permute-start.3
  42.6 1.3 collective-permute-start.4
  48.3 4.9 %collective-permute-start.5 = (f32[8,256]{1,0:T(8,128)S(1)}, f32[8,256]{1,0:T(8,128)S(1)}, u32[]{:S(2)}, u32[]{:S(2)}) collective-permute-start(f32[8,256]{1,0:T(8,128)S(1)} %get-tuple-element.38.p0), channel_id=1, source_target_pairs={{0,1},{1,2},{2,3},{3,0},{4,5},{5,6},{6,7},{7,4},{8,9},{9,10},{10,1... | collective-permute-start | bytes 24584 | tf_op jit(solution)/shard_map/ppermute | solution.py:454
  48.4 4.9 %collective-permute-start.6 = (f32[8,256]{1,0:T(8,128)S(1)}, f32[8,256]{1,0:T(8,128)S(1)}, u32[]{:S(2)}, u32[]{:S(2)}) collective-permute-start(f32[8,256]{1,0:T(8,128)S(1)} %get-tuple-element.38.p0), channel_id=1, source_target_pairs={{0,3},{1,0},{2,1},{3,2},{4,7},{5,4},{6,5},{7,6},{8,11},{9,8},{10,9... | collective-permute-start | bytes 24584 | tf_op jit(solution)/shard_map/ppermute | solution.py:454
  51.6 5.2 %collective-permute-start.7 = (f32[8,256]{1,0:T(8,128)S(1)}, f32[8,256]{1,0:T(8,128)S(1)}, u32[]{:S(2)}, u32[]{:S(2)}) collective-permute-start(f32[8,256]{1,0:T(8,128)S(1)} %get-tuple-element.38.p0), channel_id=1, source_target_pairs={{0,2},{1,3},{2,0},{3,1},{4,6},{5,7},{6,4},{7,5},{8,10},{9,11},{10,... | collective-permute-start | bytes 24584 | tf_op jit(solution)/shard_map/ppermute | solution.py:454
  59.7 1.3 collective-permute-start.8
  74.8 1.3 collective-permute-start.9
  79.4 4.9 %collective-permute-start.10 = (f32[8,256]{1,0:T(8,128)S(1)}, f32[8,256]{1,0:T(8,128)S(1)}, u32[]{:S(2)}, u32[]{:S(2)}) collective-permute-start(f32[8,256]{1,0:T(8,128)S(1)} %shard_map.81.p0), channel_id=1, source_target_pairs={{0,1},{1,2},{2,3},{3,0},{4,5},{5,6},{6,7},{7,4},{8,9},{9,10},{10,1... | collective-permute-start | bytes 24584 | tf_op jit(solution)/shard_map/ppermute | solution.py:454
  79.5 4.9 %collective-permute-start.11 = (f32[8,256]{1,0:T(8,128)S(1)}, f32[8,256]{1,0:T(8,128)S(1)}, u32[]{:S(2)}, u32[]{:S(2)}) collective-permute-start(f32[8,256]{1,0:T(8,128)S(1)} %shard_map.81.p0), channel_id=1, source_target_pairs={{0,3},{1,0},{2,1},{3,2},{4,7},{5,4},{6,5},{7,6},{8,11},{9,8},{10,9... | collective-permute-start | bytes 24584 | tf_op jit(solution)/shard_map/ppermute | solution.py:454
  82.7 5.2 %collective-permute-start.12 = (f32[8,256]{1,0:T(8,128)S(1)}, f32[8,256]{1,0:T(8,128)S(1)}, u32[]{:S(2)}, u32[]{:S(2)}) collective-permute-start(f32[8,256]{1,0:T(8,128)S(1)} %shard_map.81.p0), channel_id=1, source_target_pairs={{0,2},{1,3},{2,0},{3,1},{4,6},{5,7},{6,4},{7,5},{8,10},{9,11},{10,... | collective-permute-start | bytes 24584 | tf_op jit(solution)/shard_map/ppermute | solution.py:454
  97.6 4.5 %collective-permute-start.21 = (f32[4,8,32,512]{3,2,1,0:T(8,128)}, f32[4,8,32,512]{3,2,1,0:T(8,128)S(1)}, u32[]{:S(2)}, u32[]{:S(2)}) collective-permute-start(f32[4,8,32,512]{3,2,1,0:T(8,128)} %get-tuple-element.53), channel_id=1, source_target_pairs={{0,4},{4,0},{1,5},{5,1},{2,6},{6,2},{3,7},{7,3},{8,12},{12,8},{9,1... | collective-permute-start | bytes 6291464 | tf_op jit(solution)/shard_map/ppermute | solution.py:454
  102.3 12.0 %collective-permute-start.22 = (f32[4,32,512]{2,1,0:T(8,128)S(1)}, f32[4,32,512]{2,1,0:T(8,128)S(1)}, u32[]{:S(2)}, u32[]{:S(2)}) collective-permute-start(f32[4,32,512]{2,1,0:T(8,128)S(1)} %get-tuple-element.56), channel_id=1, source_target_pairs={{0,64},{64,128},{128,192},{192,0},{1,65},{65,129},{129,193},{193,1... | collective-permute-start | bytes 786440 | tf_op jit(solution)/shard_map/ppermute | solution.py:454
  102.4 1.3 collective-permute-start.13
  104.3 16.2 %all-to-all-start.2 = ((f32[32,8,128]{2,1,0:T(8,128)}), f32[32,8,128]{2,1,0:T(8,128)S(1)}, u32[]{:S(2)}, u32[]{:S(2)}) async-start(f32[32,8,128]{2,1,0:T(8,128)} %broadcast_in_dim.8), calls=%async_computation.2 | async-start | bytes 262144 | tf_op jit(solution)/shard_map/all_to_all | solution.py:465
  110.9 10.5 %collective-permute-start.26 = (f32[4,32,512]{2,1,0:T(8,128)S(1)}, f32[4,32,512]{2,1,0:T(8,128)S(1)}, u32[]{:S(2)}, u32[]{:S(2)}) collective-permute-start(f32[4,32,512]{2,1,0:T(8,128)S(1)} %get-tuple-element.61), channel_id=1, source_target_pairs={{0,192},{64,0},{128,64},{192,128},{1,193},{65,1},{129,65},{193,129... | collective-permute-start | bytes 786440 | tf_op jit(solution)/shard_map/ppermute | solution.py:454
  111.2 15.9 %collective-permute-start.24 = (f32[4,32,512]{2,1,0:T(8,128)S(1)}, f32[4,32,512]{2,1,0:T(8,128)}, u32[]{:S(2)}, u32[]{:S(2)}) collective-permute-start(f32[4,32,512]{2,1,0:T(8,128)S(1)} %get-tuple-element.57), channel_id=1, source_target_pairs={{0,192},{64,0},{128,64},{192,128},{1,193},{65,1},{129,65},{193,129... | collective-permute-start | bytes 786440 | tf_op jit(solution)/shard_map/ppermute | solution.py:454
  114.3 14.4 %collective-permute-start.23 = (f32[4,32,512]{2,1,0:T(8,128)S(1)}, f32[4,32,512]{2,1,0:T(8,128)}, u32[]{:S(2)}, u32[]{:S(2)}) collective-permute-start(f32[4,32,512]{2,1,0:T(8,128)S(1)} %add.49), channel_id=1, source_target_pairs={{0,64},{64,128},{128,192},{192,0},{1,65},{65,129},{129,193},{193,1... | collective-permute-start | bytes 786440 | tf_op jit(solution)/shard_map/ppermute | solution.py:454
  120.5 2.2 %collective-permute-start.14 = (f32[32,8,128]{2,1,0:T(8,128)S(1)}, f32[32,8,128]{2,1,0:T(8,128)S(1)}, u32[]{:S(2)}, u32[]{:S(2)}) collective-permute-start(f32[32,8,128]{2,1,0:T(8,128)S(1)} %all-to-all-done.2.mine), channel_id=1, source_target_pairs={{0,4},{4,0},{1,5},{5,1},{2,6},{6,2},{3,7},{7,3},{8,12},{12,8},{9,1... | collective-permute-start | bytes 393224 | tf_op jit(solution)/shard_map/ppermute | solution.py:454
  120.5 9.4 %collective-permute-start.25 = (f32[4,32,512]{2,1,0:T(8,128)S(1)}, f32[4,32,512]{2,1,0:T(8,128)S(1)}, u32[]{:S(2)}, u32[]{:S(2)}) collective-permute-start(f32[4,32,512]{2,1,0:T(8,128)S(1)} %get-tuple-element.59), channel_id=1, source_target_pairs={{0,64},{64,128},{128,192},{192,0},{1,65},{65,129},{129,193},{193,1... | collective-permute-start | bytes 786440 | tf_op jit(solution)/shard_map/ppermute | solution.py:454
  121.5 10.0 %collective-permute-start.27 = (f32[4,32,512]{2,1,0:T(8,128)S(1)}, f32[4,32,512]{2,1,0:T(8,128)S(1)}, u32[]{:S(2)}, u32[]{:S(2)}) collective-permute-start(f32[4,32,512]{2,1,0:T(8,128)S(1)} %add.53), channel_id=1, source_target_pairs={{0,192},{64,0},{128,64},{192,128},{1,193},{65,1},{129,65},{193,129... | collective-permute-start | bytes 786440 | tf_op jit(solution)/shard_map/ppermute | solution.py:454
  126.7 20.2 %collective-permute-start.19 = (f32[264,512]{1,0:T(8,128)S(1)}, f32[264,512]{1,0:T(8,128)}, u32[]{:S(2)}, u32[]{:S(2)}) collective-permute-start(f32[264,512]{1,0:T(8,128)S(1)} %get-tuple-element.51), channel_id=1, source_target_pairs={{0,3},{1,0},{2,1},{3,2},{4,7},{5,4},{6,5},{7,6},{8,11},{9,8},{10,9... | collective-permute-start | bytes 1622024 | tf_op jit(solution)/shard_map/ppermute | solution.py:454
  127.1 22.6 %collective-permute-start.15 = (f32[264,512]{1,0:T(8,128)S(1)}, f32[264,512]{1,0:T(8,128)S(1)}, u32[]{:S(2)}, u32[]{:S(2)}) collective-permute-start(f32[264,512]{1,0:T(8,128)S(1)} %get-tuple-element.46), channel_id=1, source_target_pairs={{0,1},{1,2},{2,3},{3,0},{4,5},{5,6},{6,7},{7,4},{8,9},{9,10},{10,1... | collective-permute-start | bytes 1622024 | tf_op jit(solution)/shard_map/ppermute | solution.py:454
  132.4 41.7 %all-to-all-start.3 = ((f32[8,32,512]{2,1,0:T(8,128)}), f32[8,32,512]{2,1,0:T(8,128)S(1)}, u32[]{:S(2)}, u32[]{:S(2)}) async-start(f32[8,32,512]{2,1,0:T(8,128)} %pad_maximum_fusion), calls=%async_computation.3 | async-start | bytes 1048576 | tf_op jit(solution)/shard_map/all_to_all | solution.py:585
  144.8 15.2 %collective-permute-start.17 = (f32[264,512]{1,0:T(8,128)S(1)}, f32[264,512]{1,0:T(8,128)S(1)}, u32[]{:S(2)}, u32[]{:S(2)}) collective-permute-start(f32[264,512]{1,0:T(8,128)S(1)} %get-tuple-element.47), channel_id=1, source_target_pairs={{0,3},{1,0},{2,1},{3,2},{4,7},{5,4},{6,5},{7,6},{8,11},{9,8},{10,9... | collective-permute-start | bytes 1622024 | tf_op jit(solution)/shard_map/ppermute | solution.py:454
  145.3 16.6 %collective-permute-start.18 = (f32[264,512]{1,0:T(8,128)}, f32[264,512]{1,0:T(8,128)S(1)}, u32[]{:S(2)}, u32[]{:S(2)}) collective-permute-start(f32[264,512]{1,0:T(8,128)} %get-tuple-element.49), channel_id=1, source_target_pairs={{0,1},{1,2},{2,3},{3,0},{4,5},{5,6},{6,7},{7,4},{8,9},{9,10},{10,1... | collective-permute-start | bytes 1622024 | tf_op jit(solution)/shard_map/ppermute | solution.py:454
  148.1 22.8 %collective-permute-start.20 = (f32[264,512]{1,0:T(8,128)S(1)}, f32[264,512]{1,0:T(8,128)S(1)}, u32[]{:S(2)}, u32[]{:S(2)}) collective-permute-start(f32[264,512]{1,0:T(8,128)S(1)} %add.48), channel_id=1, source_target_pairs={{0,3},{1,0},{2,1},{3,2},{4,7},{5,4},{6,5},{7,6},{8,11},{9,8},{10,9... | collective-permute-start | bytes 1622024 | tf_op jit(solution)/shard_map/ppermute | solution.py:454
  149.8 22.9 %collective-permute-start.16 = (f32[264,512]{1,0:T(8,128)S(1)}, f32[264,512]{1,0:T(8,128)S(1)}, u32[]{:S(2)}, u32[]{:S(2)}) collective-permute-start(f32[264,512]{1,0:T(8,128)S(1)} %add.47), channel_id=1, source_target_pairs={{0,1},{1,2},{2,3},{3,0},{4,5},{5,6},{6,7},{7,4},{8,9},{9,10},{10,1... | collective-permute-start | bytes 1622024 | tf_op jit(solution)/shard_map/ppermute | solution.py:454
